TPU v7x, 512 devices: a whole 4x8x8 slice. The times are simulated.
512 devices in a mesh: seq: 128 (over z, y, core), head: 4 (over x).
Axes of the slice: x: 4, y: 8, z: 8, core: 2. Of those that a mesh axis runs over, the one named last changes fastest.
Arguments:
- queries: bfloat16 [32768, 4096], P('seq', 'head'), may hold values from -6 to 6
- keys: bfloat16 [32768, 512], P(('seq', 'head')), may hold values from -6 to 6
- values: bfloat16 [32768, 512], P(('seq', 'head')), may hold values from -6 to 6
- d_out: bfloat16 [32768, 4096], P('seq', 'head'), may hold values from -6 to 6
- rand_blocks: int32 [512, 8], P('seq'), may hold values from 0 to 511, as said below
- glob_blocks: int32 [2], replicated, may hold values from 0 to 511
Outputs:
- attn_out: bfloat16 [32768, 4096], P('seq', 'head')
- d_queries: bfloat16 [32768, 4096], P('seq', 'head')
- d_keys: bfloat16 [32768, 512], P(('seq', 'head'))
- d_values: bfloat16 [32768, 512], P(('seq', 'head'))
Inputs may be any that keep to these rules, and one draw needn't show every extreme that they name: `rand_blocks`: block b lies on index b // 4 of seq. Among the 32 entries of the query blocks of one index of seq, at most 1 name blocks of any one index, and some index of seq reaches 1 for some owner in every draw.
All inputs are finite; a program needn't handle non-finite values.
Results may differ from a plain program's by a relative error of at most 0.012.
Values may be sent and summed in bfloat16 or wider, within the bound.
A program may use at most 64 MiB of HBM per device.

v0:
```python
import jax
import jax.numpy as jnp
from jax import lax
from jax.sharding import PartitionSpec as P

DH = 128
KVH = 4
BLOCK = 64
GLOB = 2
RAND = 8


NEG_FILL = -1e30


def padded_2(cells, sides, width):
    for axis, dim in sides:
        count = lax.axis_size(axis)
        ends = count - 1
        head = lax.slice_in_dim(cells, 0, width, axis=dim)
        tail = lax.slice_in_dim(cells, cells.shape[dim] - width, cells.shape[dim], axis=dim)
        cells = jnp.concatenate(
            [
                lax.ppermute(tail, axis, [(i, (i + 1) % count) for i in range(ends)]),
                cells,
                lax.ppermute(head, axis, [((i + 1) % count, i) for i in range(ends)]),
            ],
            axis=dim,
        )
    return cells


def broadcast(block, axis, source):
    block = jnp.where(lax.axis_index(axis) == source, block, jnp.zeros_like(block))
    return lax.psum(block, axis)


def key_rows(library, spots):
    chosen = library[spots]
    flat = chosen.reshape(chosen.shape[0] * chosen.shape[1], chosen.shape[2])
    return (flat[:, :DH], flat[:, DH:])


def masked_scores(query_block, keys_here, allowed_row):
    factor = DH ** (-0.5)
    scores = (
        jnp.einsum("thd,kd->htk", query_block, keys_here, preferred_element_type=jnp.float32)
        * factor
    )
    widened = jnp.repeat(allowed_row, keys_here.shape[0] // allowed_row.shape[0])
    return jnp.where(widened[None, None, :], scores, NEG_FILL)


def body(queries, keys, values, d_out, rand_blocks, glob_blocks):
    seq_count = lax.axis_size("seq")
    here = lax.axis_index("seq")
    short = keys.shape[0]
    stacked = jnp.concatenate(
        [keys.reshape(short, KVH, DH), values.reshape(short, KVH, DH)], axis=2
    )
    mine = lax.all_to_all(stacked, "head", split_axis=1, concat_axis=0, tiled=True)
    tok_count = mine.shape[0]
    blocks_here = tok_count // BLOCK
    flat_pairs = mine.reshape(tok_count, 2 * DH)
    own_blocks = flat_pairs.reshape(blocks_here, BLOCK, 2 * DH)
    padded = padded_2(flat_pairs, (("seq", 0),), BLOCK)
    window = padded.reshape(blocks_here + 2, BLOCK, 2 * DH)
    global_parts = []
    for number in range(GLOB):
        target = glob_blocks[number]
        piece = lax.dynamic_index_in_dim(own_blocks, target % blocks_here, 0, keepdims=False)
        global_parts.append(broadcast(piece, "seq", target // blocks_here))
    global_pairs = jnp.stack(global_parts)
    entries = rand_blocks.reshape(-1)
    entry_count = entries.shape[0]
    capacity = -(-entry_count // seq_count)
    position_count = seq_count * capacity
    owners = entries // blocks_here
    inner_index = entries % blocks_here
    order = jnp.arange(entry_count, dtype=jnp.int32)
    earlier = (owners[:, None] == owners[None, :]) & (order[:, None] > order[None, :])
    ranks = jnp.sum(earlier.astype(jnp.int32), axis=1)
    slots = owners * capacity + ranks
    placing = slots[None, :] == jnp.arange(position_count, dtype=jnp.int32)[:, None]
    wanted = jnp.sum(jnp.where(placing, inner_index[None, :], 0), axis=1).reshape(
        seq_count, capacity
    )
    incoming = lax.all_to_all(wanted, "seq", split_axis=0, concat_axis=0, tiled=True).reshape(
        position_count
    )
    served = own_blocks[incoming].reshape(seq_count, capacity, BLOCK, 2 * DH)
    fetched = lax.all_to_all(served, "seq", split_axis=0, concat_axis=0, tiled=True).reshape(
        position_count, BLOCK, 2 * DH
    )
    block_ids = jnp.arange(blocks_here, dtype=jnp.int32)
    window_ids = jnp.stack([block_ids, block_ids + 1, block_ids + 2], axis=1)
    global_ids = jnp.broadcast_to(
        blocks_here + 2 + jnp.arange(GLOB, dtype=jnp.int32), (blocks_here, GLOB)
    )
    random_ids = blocks_here + 2 + GLOB + slots.reshape(blocks_here, RAND)
    positions = jnp.concatenate([window_ids, global_ids, random_ids], axis=1)
    allowed = jnp.concatenate(
        [
            jnp.logical_not((block_ids == 0) & (here == 0))[:, None],
            jnp.ones((blocks_here, 1), jnp.bool_),
            jnp.logical_not((block_ids == blocks_here - 1) & (here == seq_count - 1))[:, None],
            jnp.ones((blocks_here, GLOB + RAND), jnp.bool_),
        ],
        axis=1,
    )
    library = jnp.concatenate([window, global_pairs, fetched], axis=0)
    heads_here = queries.shape[1] // DH
    query_blocks = queries.reshape(blocks_here, BLOCK, heads_here, DH)
    grad_blocks = d_out.reshape(blocks_here, BLOCK, heads_here, DH)

    def forward_step(inputs):
        query_block, spots, allowed_row = inputs
        keys_here, values_here = key_rows(library, spots)
        scores = masked_scores(query_block, keys_here, allowed_row)
        peak = jnp.max(scores, axis=-1, keepdims=True)
        logsum = peak + jnp.log(jnp.sum(jnp.exp(scores - peak), axis=-1, keepdims=True))
        probs16 = jnp.exp(scores - logsum).astype(jnp.bfloat16)
        result = jnp.einsum("htk,kd->thd", probs16, values_here, preferred_element_type=jnp.float32)
        return (result.astype(jnp.bfloat16), logsum)

    out_blocks, logsums = lax.map(forward_step, (query_blocks, positions, allowed))
    refetched = lax.all_to_all(served, "seq", split_axis=0, concat_axis=0, tiled=True).reshape(
        position_count, BLOCK, 2 * DH
    )
    library_back = jnp.concatenate([window, global_pairs, refetched], axis=0)

    def backward_step(inputs):
        query_block, gradient_tile, out_block, logsum, spots, allowed_row = inputs
        keys_here, values_here = key_rows(library_back, spots)
        factor = DH ** (-0.5)
        scores = masked_scores(query_block, keys_here, allowed_row)
        probs = jnp.exp(scores - logsum)
        probs16 = probs.astype(jnp.bfloat16)
        delta = jnp.sum(gradient_tile.astype(jnp.float32) * out_block.astype(jnp.float32), axis=-1)
        dprobs = jnp.einsum(
            "thd,kd->htk", gradient_tile, values_here, preferred_element_type=jnp.float32
        )
        dscores = (probs * (dprobs - jnp.transpose(delta)[:, :, None])).astype(jnp.bfloat16)
        dquery = (
            jnp.einsum("htk,kd->thd", dscores, keys_here, preferred_element_type=jnp.float32)
            * factor
        )
        dkey = (
            jnp.einsum("htk,thd->kd", dscores, query_block, preferred_element_type=jnp.float32)
            * factor
        )
        dvalue = jnp.einsum(
            "htk,thd->kd", probs16, gradient_tile, preferred_element_type=jnp.float32
        )
        terms = jnp.concatenate([dkey, dvalue], axis=1).reshape(spots.shape[0], BLOCK, 2 * DH)
        return (dquery.astype(jnp.bfloat16), terms)

    dquery_blocks, terms = lax.map(
        backward_step, (query_blocks, grad_blocks, out_blocks, logsums, positions, allowed)
    )
    attn_out = out_blocks.reshape(tok_count, heads_here * DH)
    d_queries = dquery_blocks.reshape(tok_count, heads_here * DH)
    prev_terms = terms[:, 0]
    self_terms = terms[:, 1]
    next_terms = terms[:, 2]
    zero_block = jnp.zeros((1, BLOCK, 2 * DH), jnp.float32)
    grads = (
        self_terms
        + jnp.concatenate([prev_terms[1:], zero_block], axis=0)
        + jnp.concatenate([zero_block, next_terms[:-1]], axis=0)
    )
    rims = jnp.concatenate([prev_terms[0], next_terms[-1]], axis=0).astype(jnp.bfloat16)
    arrived = padded_2(rims, (("seq", 0),), BLOCK)
    from_left = arrived[:BLOCK].astype(jnp.float32)
    from_right = arrived[3 * BLOCK :].astype(jnp.float32)
    edge_first = jnp.concatenate(
        [from_left[None], jnp.zeros((blocks_here - 1, BLOCK, 2 * DH), jnp.float32)], axis=0
    )
    edge_last = jnp.concatenate(
        [jnp.zeros((blocks_here - 1, BLOCK, 2 * DH), jnp.float32), from_right[None]], axis=0
    )
    grads = grads + edge_first + edge_last
    global_terms = jnp.sum(terms[:, 3 : 3 + GLOB], axis=0)
    global_total = lax.psum(global_terms, "seq")
    global_hits = ((glob_blocks // blocks_here)[:, None] == here) & (
        (glob_blocks % blocks_here)[:, None] == block_ids[None, :]
    )
    grads = grads + jnp.sum(
        jnp.where(global_hits[:, :, None, None], global_total[:, None], 0.0), axis=0
    )
    random_terms = terms[:, 3 + GLOB :].reshape(entry_count, BLOCK * 2 * DH).astype(jnp.bfloat16)
    outgoing = jnp.dot(
        placing.astype(jnp.bfloat16), random_terms, preferred_element_type=jnp.float32
    ).astype(jnp.bfloat16)
    returned = lax.all_to_all(
        outgoing.reshape(seq_count, capacity, BLOCK, 2 * DH),
        "seq",
        split_axis=0,
        concat_axis=0,
        tiled=True,
    )
    landing = (incoming[None, :] == block_ids[:, None]).astype(jnp.bfloat16)
    grads = grads + jnp.dot(
        landing,
        returned.reshape(position_count, BLOCK * 2 * DH),
        preferred_element_type=jnp.float32,
    ).reshape(blocks_here, BLOCK, 2 * DH)
    packed = grads.astype(jnp.bfloat16).reshape(tok_count, 1, 2 * DH)
    restored = lax.all_to_all(packed, "head", split_axis=0, concat_axis=1, tiled=True)
    d_keys = restored[:, :, :DH].reshape(short, KVH * DH)
    d_values = restored[:, :, DH:].reshape(short, KVH * DH)
    return (attn_out, d_queries, d_keys, d_values)


def solution(mesh):
    in_specs = (
        P("seq", "head"),
        P(("seq", "head"), None),
        P(("seq", "head"), None),
        P("seq", "head"),
        P("seq", None),
        P(),
    )
    out_specs = (
        P("seq", "head"),
        P("seq", "head"),
        P(("seq", "head"), None),
        P(("seq", "head"), None),
    )
    return jax.shard_map(body, mesh=mesh, in_specs=in_specs, out_specs=out_specs, check_vma=False)
```

profile of v0, /device:TPU:1, one launch (start us, length us, event | category | flops | bytes accessed | tf_op | source)
XLA Modules:
  0.0 672.8 jit_solution(9760338004758471083)
XLA Ops:
  9.0 18.4 %all-to-all-start.1 = ((s32[128,1,1]{2,1,0:T(1,128)}), s32[128,1,1]{2,1,0:T(1,128)S(1)}, u32[]{:S(2)}, u32[]{:S(2)}) async-start(s32[128,1,1]{2,1,0:T(1,128)} %copy.90), calls=%async_computation.1 | async-start | bytes 131072 | tf_op jit(solution)/shard_map/all_to_all | solution.py:88
  29.0 9.9 %all-to-all-done.1 = s32[128,1,1]{2,1,0:T(1,128)S(1)} async-done(((s32[128,1,1]{2,1,0:T(1,128)}), s32[128,1,1]{2,1,0:T(1,128)S(1)}, u32[]{:S(2)}, u32[]{:S(2)}) %all-to-all-start.1) | async-done | bytes 544 | tf_op jit(solution)/shard_map/all_to_all | solution.py:88
  38.9 4.0 all-to-all-start
  45.2 2.5 all-to-all-done
  47.7 2.8 gather_fusion.2
  50.5 8.4 %all-to-all-start.2 = ((bf16[128,1,64,256]{3,2,1,0:T(8,128)(2,1)}), bf16[128,1,64,256]{3,2,1,0:T(8,128)(2,1)}, u32[]{:S(2)}, u32[]{:S(2)}) async-start(bf16[128,1,64,256]{3,2,1,0:T(8,128)(2,1)} %bitcast.301), calls=%async_computation.2 | async-start | bytes 8388608 | tf_op jit(solution)/shard_map/all_to_all | solution.py:92
  65.6 3.5 collective-permute-start
  72.0 72.9 %collective-permute-done = bf16[64,256]{1,0:T(8,128)(2,1)S(1)} collective-permute-done((bf16[64,256]{1,0:T(8,128)(2,1)S(1)}, bf16[64,256]{1,0:T(8,128)(2,1)S(1)}, u32[]{:S(2)}, u32[]{:S(2)}) %collective-permute-start) | collective-permute-done | bytes 32800 | tf_op jit(solution)/shard_map/ppermute | solution.py:24
  144.8 7.2 %collective-permute-done.1 = bf16[64,256]{1,0:T(8,128)(2,1)S(1)} collective-permute-done((bf16[64,256]{1,0:T(8,128)(2,1)S(1)}, bf16[64,256]{1,0:T(8,128)(2,1)S(1)}, u32[]{:S(2)}, u32[]{:S(2)}) %collective-permute-start.1) | collective-permute-done | bytes 32800 | tf_op jit(solution)/shard_map/ppermute | solution.py:26
  152.1 164.7 %all-reduce.10.cloned.1.call-done = (bf16[1,64,256]{2,1,0:T(8,128)(2,1)}, bf16[1,64,256]{2,1,0:T(8,128)(2,1)}) async-done(((bf16[1,64,256]{2,1,0:T(8,128)(2,1)}, bf16[1,64,256]{2,1,0:T(8,128)(2,1)}), (bf16[1,64,256]{2,1,0:T(8,128)(2,1)}, bf16[1,64,256]{2,1,0:T(8,128)(2,1)})) %all-reduce.10.cloned.1.call-update) | async-done | bytes 65552 | tf_op jit(solution)/shard_map/psum | solution.py:35
  316.8 3.9 pad_maximum_fusion.1
  320.6 18.4 %while.24 = (s32[]{:T(128)}, bf16[4,64,8,128]{3,1,2,0:T(8,128)(2,1)S(1)}, f32[4,8,64,1]{2,1,3,0:T(8,128)S(1)}, s32[4,13]{1,0:T(4,128)S(1)}, bf16[136,64,256]{2,1...) while((s32[]{:T(128)}, ...), condition=%wide.region_7.8_spmd, body=%wide.region_4.7_spmd.sunk | while | flops 221151776 | bytes 6817576 | solution.py:126
  320.8 2.8 gather_fusion
  325.4 2.8 gather_fusion
  330.0 2.8 gather_fusion
  334.6 2.8 gather_fusion
  339.0 29.0 %while.25 = (s32[]{:T(128)}, bf16[4,64,8,128]{3,2,1,0:T(8,128)(2,1)}, f32[4,13,64,256]{3,2,1,0:T(8,128)}, s32[4,13]{1,0:T(4,128)S(1)}, bf16[136,64,256]{2,1,0:T(...) while((s32[]{:T(128)}, ...), condition=%wide.region_10.11_spmd, body=%wide.region_8.10_spmd.sunk | while | flops 548954624 | bytes 15144784 | solution.py:158
  339.4 2.8 gather_fusion.1
  346.7 2.8 gather_fusion.1
  354.0 2.8 gather_fusion.1
  361.2 2.8 gather_fusion.1
  372.5 3.2 copy.125
  375.8 6.8 %all-to-all-start.3 = ((bf16[128,1,64,256]{3,2,1,0:T(8,128)(2,1)}), bf16[128,1,64,256]{3,2,1,0:T(8,128)(2,1)}, u32[]{:S(2)}, u32[]{:S(2)}) async-start(bf16[128,1,64,256]{3,2,1,0:T(8,128)(2,1)} %bitcast.302), calls=%async_computation.3 | async-start | bytes 8388608 | tf_op jit(solution)/shard_map/all_to_all | solution.py:195
  382.7 4.0 copy.97
  388.2 3.2 collective-permute-start.2
  394.7 74.3 %collective-permute-done.2 = bf16[64,256]{1,0:T(8,128)(2,1)S(1)} collective-permute-done((bf16[64,256]{1,0:T(8,128)(2,1)S(1)}, bf16[64,256]{1,0:T(8,128)(2,1)S(1)}, u32[]{:S(2)}, u32[]{:S(2)}) %collective-permute-start.2) | collective-permute-done | bytes 32800 | tf_op jit(solution)/shard_map/ppermute | solution.py:24
  469.0 6.2 collective-permute-done.3
  475.3 166.2 %all-reduce.8.cloned.1.call-done = f32[2,64,256]{2,1,0:T(8,128)} async-done(((f32[2,64,256]{2,1,0:T(8,128)}), f32[2,64,256]{2,1,0:T(8,128)}) %all-reduce.8.cloned.1.call-update) | async-done | bytes 131088 | tf_op jit(solution)/shard_map/psum | solution.py:184
  642.5 6.9 %copy.109 = bf16[128,1,64,256]{0,3,2,1:T(8,128)(2,1)} copy(bf16[128,1,64,256]{3,2,1,0:T(8,128)(2,1)} %all-to-all-done.3) | data formatting | bytes 8388608 | tf_op jit(solution)/shard_map/reshape | solution.py:205
  649.5 3.5 fusion.35
  654.9 4.0 all-to-all-start.4
  661.0 3.5 all-to-all-done.4
  (187 shorter events, 50.1 us)
Async XLA Ops:
  7.2 20.3 %copy-start = (bf16[64,512]{1,0:T(8,128)(2,1)S(1)}, bf16[64,512]{1,0:T(8,128)(2,1)}, u32[]{:S(2)}) copy-start(bf16[64,512]{1,0:T(8,128)(2,1)} %param.11) | copy-start | bytes 196612
  9.0 29.8 %all-to-all-start.1 = ((s32[128,1,1]{2,1,0:T(1,128)}), s32[128,1,1]{2,1,0:T(1,128)S(1)}, u32[]{:S(2)}, u32[]{:S(2)}) async-start(s32[128,1,1]{2,1,0:T(1,128)} %copy.90), calls=%async_computation.1 | async-start | bytes 131072 | tf_op jit(solution)/shard_map/all_to_all | solution.py:88
  38.9 8.8 %all-to-all-start = ((bf16[64,4,256]{2,0,1:T(8,128)(2,1)}), bf16[64,4,256]{2,0,1:T(8,128)(2,1)S(1)}, u32[]{:S(2)}, u32[]{:S(2)}) async-start(bf16[64,4,256]{2,0,1:T(8,128)(2,1)} %pad_maximum_fusion.3), calls=%async_computation | async-start | bytes 262144 | tf_op jit(solution)/shard_map/all_to_all | solution.py:61
  50.5 8.5 %copy-start.9 = (s32[2]{0:T(128)S(1)}, s32[2]{0:T(128)}, u32[]{:S(2)}) copy-start(s32[2]{0:T(128)} %param.15) | copy-start | bytes 28
  50.5 14.6 %copy-start.5 = (bf16[256,1024]{1,0:T(8,128)(2,1)S(1)}, bf16[256,1024]{1,0:T(8,128)(2,1)}, u32[]{:S(2)}) copy-start(bf16[256,1024]{1,0:T(8,128)(2,1)} %param.10) | copy-start | bytes 1572868
  50.5 14.8 %copy-start.6 = (bf16[256,1024]{1,0:T(8,128)(2,1)S(1)}, bf16[256,1024]{1,0:T(8,128)(2,1)}, u32[]{:S(2)}) copy-start(bf16[256,1024]{1,0:T(8,128)(2,1)} %param.13) | copy-start | bytes 1572868
  50.5 14.9 %copy-start.8 = (s32[4,8]{1,0:T(4,128)S(1)}, s32[4,8]{1,0:T(4,128)}, u32[]{:S(2)}) copy-start(s32[4,8]{1,0:T(4,128)} %param.14) | copy-start | bytes 388
  50.5 266.3 %all-to-all-start.2 = ((bf16[128,1,64,256]{3,2,1,0:T(8,128)(2,1)}), bf16[128,1,64,256]{3,2,1,0:T(8,128)(2,1)}, u32[]{:S(2)}, u32[]{:S(2)}) async-start(bf16[128,1,64,256]{3,2,1,0:T(8,128)(2,1)} %bitcast.301), calls=%async_computation.2 | async-start | bytes 8388608 | tf_op jit(solution)/shard_map/all_to_all | solution.py:92
  58.9 257.8 %all-reduce.10.cloned.1.call-start = ((), (), s32[]{:S(2)}) async-start(), calls=%async_computation.6 | async-start | bytes 131072 | tf_op jit(solution)/shard_map/psum | solution.py:35
  65.6 79.2 %collective-permute-start = (bf16[64,256]{1,0:T(8,128)(2,1)S(1)}, bf16[64,256]{1,0:T(8,128)(2,1)S(1)}, u32[]{:S(2)}, u32[]{:S(2)}) collective-permute-start(bf16[64,256]{1,0:T(8,128)(2,1)S(1)} %get-tuple-element.230), channel_id=1, source_target_pairs={{0,4},{4,8},{8,12},{12,16},{16,20},{20,24},{24,28},{28,32},{32,36}... | collective-permute-start | bytes 98312 | tf_op jit(solution)/shard_map/ppermute | solution.py:24
  69.2 82.9 %collective-permute-start.1 = (bf16[64,256]{1,0:T(8,128)(2,1)S(1)}, bf16[64,256]{1,0:T(8,128)(2,1)S(1)}, u32[]{:S(2)}, u32[]{:S(2)}) collective-permute-start(bf16[64,256]{1,0:T(8,128)(2,1)S(1)} %get-tuple-element.231), channel_id=1, source_target_pairs={{4,0},{8,4},{12,8},{16,12},{20,16},{24,20},{28,24},{32,28},{36,32}... | collective-permute-start | bytes 98312 | tf_op jit(solution)/shard_map/ppermute | solution.py:26
  368.0 2.5 copy-start.3
  370.4 2.1 copy-start.2
  375.8 6.9 %copy-start.1 = (f32[4,13,64,256]{3,2,1,0:T(8,128)S(1)}, f32[4,13,64,256]{3,2,1,0:T(8,128)}, u32[]{:S(2)}) copy-start(f32[4,13,64,256]{3,2,1,0:T(8,128)} %get-tuple-element.98) | copy-start | bytes 10223620
  375.8 266.8 %all-to-all-start.3 = ((bf16[128,1,64,256]{3,2,1,0:T(8,128)(2,1)}), bf16[128,1,64,256]{3,2,1,0:T(8,128)(2,1)}, u32[]{:S(2)}, u32[]{:S(2)}) async-start(bf16[128,1,64,256]{3,2,1,0:T(8,128)(2,1)} %bitcast.302), calls=%async_computation.3 | async-start | bytes 8388608 | tf_op jit(solution)/shard_map/all_to_all | solution.py:195
  382.5 258.9 %all-reduce.8.cloned.1.call-start = ((), (), s32[]{:S(2)}) async-start(), calls=%async_computation.5 | async-start | bytes 262144 | tf_op jit(solution)/shard_map/psum | solution.py:184
  388.2 80.8 %collective-permute-start.2 = (bf16[64,256]{1,0:T(8,128)(2,1)S(1)}, bf16[64,256]{1,0:T(8,128)(2,1)S(1)}, u32[]{:S(2)}, u32[]{:S(2)}) collective-permute-start(bf16[64,256]{1,0:T(8,128)(2,1)S(1)} %get-tuple-element.226), channel_id=1, source_target_pairs={{0,4},{4,8},{8,12},{12,16},{16,20},{20,24},{24,28},{28,32},{32,36}... | collective-permute-start | bytes 98312 | tf_op jit(solution)/shard_map/ppermute | solution.py:24
  391.4 83.8 %collective-permute-start.3 = (bf16[64,256]{1,0:T(8,128)(2,1)S(1)}, bf16[64,256]{1,0:T(8,128)(2,1)S(1)}, u32[]{:S(2)}, u32[]{:S(2)}) collective-permute-start(bf16[64,256]{1,0:T(8,128)(2,1)S(1)} %get-tuple-element.227), channel_id=1, source_target_pairs={{4,0},{8,4},{12,8},{16,12},{20,16},{24,20},{28,24},{32,28},{36,32}... | collective-permute-start | bytes 98312 | tf_op jit(solution)/shard_map/ppermute | solution.py:26
  649.4 9.4 %copy-start.4 = (bf16[4,64,8,128]{3,1,2,0:T(8,128)(2,1)S(1)}, bf16[4,64,8,128]{3,1,2,0:T(8,128)(2,1)}, u32[]{:S(2)}) copy-start(bf16[4,64,8,128]{3,1,2,0:T(8,128)(2,1)} %copy-done.3) | copy-start | bytes 1572868
  649.5 9.7 %copy-start.7 = (bf16[4,64,8,128]{3,2,1,0:T(8,128)(2,1)S(1)}, bf16[4,64,8,128]{3,2,1,0:T(8,128)(2,1)}, u32[]{:S(2)}) copy-start(bf16[4,64,8,128]{3,2,1,0:T(8,128)(2,1)} %get-tuple-element.97) | copy-start | bytes 1572868
  654.9 9.6 %all-to-all-start.4 = ((bf16[4,2,8192]{2,1,0:T(2,128)(2,1)}), bf16[4,2,8192]{2,1,0:T(2,128)(2,1)S(1)}, u32[]{:S(2)}, u32[]{:S(2)}) async-start(bf16[4,2,8192]{2,1,0:T(2,128)(2,1)} %reshape.443), calls=%async_computation.4 | async-start | bytes 262144 | tf_op jit(solution)/shard_map/all_to_all | solution.py:209
Sparse Core Ops, SparseCore 0:
  72.1 244.6 all-reduce.9
  387.5 253.9 all-reduce.7
where the time goes:
time: 674 us; the launch traced here: 673 us
  waiting for transfers between devices  507 us (75%)
  local copies, waits for them, and re-layouts  59.1 us (9%)
  starting transfers between devices  52.7 us (8%)
  between operations  19.6 us (3%)
  matrix products  17.9 us (3%)
  other arithmetic  15.6 us (2%)
    psum x1, waiting for transfers between devices, body(): global_total = lax.psum(global_terms, 'seq')  166 us
    psum x1, waiting for transfers between devices, broadcast(): return lax.psum(block, axis)  165 us
    ppermute x2, waiting for transfers between devices, padded_2(): lax.ppermute(tail, axis, [(i, (i + 1) % count) for i in range(ends)])  147 us
    gather x8, local copies, waits for them, and re-layouts, key_rows(): chosen = library[spots]  22.7 us
    all_to_all x1, starting transfers between devices, body(): lax.all_to_all(wanted, 'seq', split_axis=0, concat_axis=0, tiled=True)  18.4 us
  transfers between devices with their start and end apart: 11, of which 9 were waited for; matrix products, arithmetic and copies ran while one was open for 2% of the time, Pallas kernels for 0%

commit v1 on v0

v1 whole, which is shorter than its diff:
```python
import functools

import jax
import jax.numpy as jnp
from jax import lax
from jax.experimental import pallas as pl
from jax.experimental.pallas import tpu as pltpu
from jax.sharding import PartitionSpec as P

DH = 128
KVH = 4
HEADS = 8
BLOCK = 64
RAND = 8
PAIR = 2 * DH
RING = 8
NEG_FILL = -1e30
BF16 = jnp.bfloat16
F32 = jnp.float32
MESH = pl.DeviceIdType.MESH

ORDER = (0, 1, -1, 2, -2, 3, -3, 4)
SLOT = {d: i for i, d in enumerate(ORDER)}
UNITS = ((0, 1), (1, 3), (3, 5), (5, 7), (7, 8))
UNIT_OF = {d: u for u, (lo, hi) in enumerate(UNITS) for d in ORDER[lo:hi]}
FAR = {1: (0, 1, 4), -1: (2, 3)}
GROUPS = ((0, 3), (3, 7), (7, 8))
CHUNK_US = 1.41
PARTNER_US = 0.25
HOP_US = 1.7
ROWS = 40
NONE_ROW = 36


def axis_of(half, major):
    return "zy"[half] if major else "yz"[half]


def ordered(tasks):
    arrival, free, result = {}, {}, []
    waiting = list(tasks)
    while waiting:
        best = None
        for task in waiting:
            if all(dep in arrival for dep in task[3]):
                ready = max([arrival[dep] for dep in task[3]], default=0.0)
                if best is None or ready < best[0]:
                    best = (ready, task)
        ready, task = best
        waiting.remove(task)
        name, link, time, deps = task
        end = max(ready, free.get(link, 0.0)) + time
        free[link] = end
        arrival[name] = end + HOP_US
        result.append(task)
    return result, max(arrival.values())


def gather_tasks():
    tasks = []
    delivered = {}
    for half in (0, 1):
        minor, major = axis_of(half, False), axis_of(half, True)
        for sign, ends in ((1, (0, 1, 2, 3)), (-1, (0, -1, -2))):
            for d in ends:
                name = ("m", half, sign, d)
                deps = () if d == 0 else (("m", half, sign, d - sign),)
                tasks.append((name, (minor, sign), CHUNK_US, deps))
                delivered[half, 0, SLOT[d + sign]] = name
        for sign in (1, -1):
            for step in range(4):
                for u, (lo, hi) in enumerate(UNITS):
                    d = step * sign
                    if step == 3 and u not in FAR[sign]:
                        continue
                    name = ("M", half, sign, d, u)
                    if d == 0:
                        deps = tuple(delivered[half, 0, s] for s in range(lo, hi) if s)
                    else:
                        deps = (("M", half, sign, d - sign, u),)
                    tasks.append((name, (major, sign), CHUNK_US * (hi - lo), deps))
                    to = 7 if step == 3 else SLOT[d + sign]
                    for s in range(lo, hi):
                        delivered[half, to, s] = name
        for row in range(RING):
            for lo, hi in GROUPS:
                deps = tuple(
                    dict.fromkeys(delivered[half, row, s] for s in range(lo, hi) if row or s)
                )
                tasks.append((("P", half, row, lo, hi), "p", PARTNER_US * (hi - lo), deps))
    return ordered(tasks)[0]


def scatter_tasks():
    tasks = []
    for half in (0, 1):
        minor, major = axis_of(half, False), axis_of(half, True)
        for step in (4, 3, 2, 1):
            for u in (4, 3, 2, 1, 0):
                for sign in (1, -1):
                    lo, hi = UNITS[u]
                    far = u in FAR[sign]
                    if step == 4 and not far:
                        continue
                    name = ("M", half, sign, step, u)
                    deps = ()
                    if step < 3 or (step == 3 and far):
                        deps = (("M", half, sign, step + 1, u),)
                    tasks.append((name, (major, sign), CHUNK_US * (hi - lo), deps))
        for sign, top in ((1, 4), (-1, 3)):
            for step in range(top, 0, -1):
                u = UNIT_OF[step * sign]
                deps = (("M", half, 1, 1, u), ("M", half, -1, 1, u))
                if step < top:
                    deps += (("m", half, sign, step + 1),)
                tasks.append((("m", half, sign, step), (minor, sign), CHUNK_US, deps))
        deps = (("M", half, 1, 1, 0), ("M", half, -1, 1, 0), ("m", half, 1, 1), ("m", half, -1, 1))
        tasks.append((("F", half), ("f", half), 0.0, deps))
    return ordered(tasks)[0]


GATHER = gather_tasks()
SCATTER = scatter_tasks()
GATHER_SENDS = {task[0]: i for i, task in enumerate(GATHER)}
SCATTER_SENDS = {t[0]: i for i, t in enumerate(t for t in SCATTER if t[0][0] != "F")}


def place():
    seq = lax.axis_index("seq")
    head = lax.axis_index("head")
    return seq, head, seq // 16, (seq // 2) % RING, seq % 2


def neighbours(seq, head, z, y, core):
    up = lambda v: lax.rem(v + 1, RING)
    down = lambda v: lax.rem(v + RING - 1, RING)
    index = lambda zz, yy, cc: zz * 16 + yy * 2 + cc
    peers = {
        ("z", 1): index(up(z), y, core),
        ("z", -1): index(down(z), y, core),
        ("y", 1): index(z, up(y), core),
        ("y", -1): index(z, down(y), core),
        "p": index(z, y, 1 - core),
    }
    return {k: {"seq": v, "head": head} for k, v in peers.items()}


def enter(peers, seq, head):
    barrier = pltpu.get_barrier_semaphore()
    everyone = list(peers.values())
    everyone += [{"seq": seq, "head": lax.rem(head + j, KVH)} for j in (1, 2, 3)]
    for peer in everyone:
        pl.semaphore_signal(barrier, inc=1, device_id=peer, device_id_type=MESH)
    pl.semaphore_wait(barrier, len(everyone))


def remote(src, dst, send, recv, peer):
    return pltpu.make_async_remote_copy(
        src_ref=src,
        dst_ref=dst,
        send_sem=send,
        recv_sem=recv,
        device_id=peer,
        device_id_type=MESH,
    )


def gather_kernel(keys, values, rand, out, rand_out, send, recv, xsend, xrecv, isem, lsem):
    seq, head, z, y, core = place()
    peers = neighbours(seq, head, z, y, core)
    enter(peers, seq, head)
    pieces = ((keys, 0), (values, DH))
    copies = []
    for j in (1, 2, 3):
        to = lax.rem(head + j, KVH)
        for n, (source, lane) in enumerate(pieces):
            copies.append(
                remote(
                    source.at[:, pl.ds(pl.multiple_of(to * DH, DH), DH)],
                    out.at[0, head // 2, 0, lax.rem(head, 2), :, pl.ds(lane, DH)],
                    xsend.at[j - 1, n],
                    xrecv.at[j - 1, n],
                    {"seq": seq, "head": to},
                )
            )
            copies[-1].start()
    index_copy = remote(rand, rand_out, isem.at[0], isem.at[1], peers["p"])
    index_copy.start()
    local = []
    for n, (source, lane) in enumerate(pieces):
        local.append(
            pltpu.make_async_copy(
                source.at[:, pl.ds(pl.multiple_of(head * DH, DH), DH)],
                out.at[0, head // 2, 0, lax.rem(head, 2), :, pl.ds(lane, DH)],
                lsem.at[n],
            )
        )
        local[-1].start()
    for copy in local:
        copy.wait()
    for copy in copies:
        copy.wait_recv()

    started = {}
    waited = set()
    for name, link, _, deps in GATHER:
        for dep in deps:
            if dep not in waited:
                waited.add(dep)
                started[dep].wait_recv()
        half = name[1]
        if name[0] == "m":
            _, _, sign, d = name
            src = out.at[0, half, 0, pl.ds(2 * SLOT[d], 2)]
            dst = out.at[0, half, 0, pl.ds(2 * SLOT[d + sign], 2)]
        elif name[0] == "M":
            _, _, sign, d, u = name
            lo, hi = UNITS[u]
            to = 7 if abs(d) == 3 else SLOT[d + sign]
            src = out.at[0, half, SLOT[d], pl.ds(2 * lo, 2 * (hi - lo))]
            dst = out.at[0, half, to, pl.ds(2 * lo, 2 * (hi - lo))]
        else:
            _, _, row, lo, hi = name
            src = out.at[0, half, row, pl.ds(2 * lo, 2 * (hi - lo))]
            dst = out.at[1, half, row, pl.ds(2 * lo, 2 * (hi - lo))]
        i = GATHER_SENDS[name]
        copy = remote(src, dst, send.at[i], recv.at[i], peers[link])
        copy.start()
        started[name] = copy
    for name, copy in started.items():
        if name not in waited:
            copy.wait_recv()
    for copy in copies:
        copy.wait_send()
    for copy in started.values():
        copy.wait_send()
    index_copy.wait()


def gather_all(keys, values, rand):
    count = len(GATHER)
    return pl.pallas_call(
        gather_kernel,
        out_shape=(
            jax.ShapeDtypeStruct((2, 2, RING, 2 * RING, BLOCK, PAIR), BF16),
            jax.ShapeDtypeStruct(rand.shape, jnp.int32),
        ),
        in_specs=[pl.BlockSpec(memory_space=pltpu.VMEM)] * 3,
        out_specs=(pl.BlockSpec(memory_space=pl.ANY), pl.BlockSpec(memory_space=pltpu.VMEM)),
        scratch_shapes=[
            pltpu.SemaphoreType.DMA((count,)),
            pltpu.SemaphoreType.DMA((count,)),
            pltpu.SemaphoreType.DMA((3, 2)),
            pltpu.SemaphoreType.DMA((3, 2)),
            pltpu.SemaphoreType.DMA((2,)),
            pltpu.SemaphoreType.DMA((2,)),
        ],
        compiler_params=pltpu.CompilerParams(collective_id=1, has_side_effects=True),
        name="gather_blocks",
    )(keys, values, rand)


def scatter_kernel(
    index, table, own, dk, dv, far, mirror, zero, line, start, final, send, recv, xsend, xrecv, psem, lsem
):
    seq, head, z, y, core = place()
    peers = neighbours(seq, head, z, y, core)
    enter(peers, seq, head)
    partner = remote(table, mirror, psem.at[0], psem.at[1], peers["p"])
    partner.start()
    partner.wait_recv()

    def local_sum(spot):
        total = table[index[0, spot]].astype(F32) + table[index[1, spot]].astype(F32)
        return total + (mirror[index[2, spot]].astype(F32) + mirror[index[3, spot]].astype(F32))

    started = {}
    waited = set()
    for name, link, _, deps in SCATTER:
        for dep in deps:
            if dep not in waited:
                waited.add(dep)
                started[dep].wait_recv()
        half = name[1]
        if name[0] == "F":

            @pl.loop(0, 2)
            def _(j):
                total = local_sum(half * 128 + j) + own[half * 2 + j]
                total += far[half, 0, j].astype(F32) + zero[half, j].astype(F32)
                total += line[half, j].astype(F32) + start[half, j].astype(F32)
                final[half * 2 + j] = total.astype(BF16)

            continue
        if name[0] == "M":
            _, _, sign, step, u = name
            lo, hi = UNITS[u]
            row = SLOT[step * sign] if step < 4 else 7
            arrived = bool(deps)

            @pl.loop(0, 2 * (hi - lo))
            def _(j):
                j = 2 * lo + j
                total = local_sum((half * 8 + row) * 16 + j)
                if arrived:
                    total += far[half, row, j].astype(F32)
                far[half, row, j] = total.astype(BF16)

            size = pl.ds(2 * lo, 2 * (hi - lo))
            src = far.at[half, row, size]
            if step > 1:
                dst = far.at[half, SLOT[(step - 1) * sign], size]
            elif sign > 0:
                dst = far.at[half, 0, size]
            else:
                dst = zero.at[half, size]
        else:
            _, _, sign, step = name
            at = 2 * SLOT[step * sign]
            arrived = len(deps) > 2

            @pl.loop(0, 2)
            def _(j):
                j = at + j
                total = local_sum(half * 128 + j)
                total += far[half, 0, j].astype(F32) + zero[half, j].astype(F32)
                if arrived:
                    total += line[half, j].astype(F32)
                line[half, j] = total.astype(BF16)

            src = line.at[half, pl.ds(at, 2)]
            if step > 1:
                dst = line.at[half, pl.ds(2 * SLOT[(step - 1) * sign], 2)]
            elif sign > 0:
                dst = line.at[half, pl.ds(0, 2)]
            else:
                dst = start.at[half]
        i = SCATTER_SENDS[name]
        copy = remote(src, dst, send.at[i], recv.at[i], peers[link[0], -link[1]])
        copy.start()
        started[name] = copy

    pieces = ((dk, 0), (dv, DH))
    here = pl.ds(pl.multiple_of(head * DH, DH), DH)
    copies = []
    for j in (1, 2, 3):
        to = lax.rem(head + j, KVH)
        for n, (target, lane) in enumerate(pieces):
            copies.append(
                remote(
                    final.at[to, :, pl.ds(lane, DH)],
                    target.at[:, here],
                    xsend.at[j - 1, n],
                    xrecv.at[j - 1, n],
                    {"seq": seq, "head": to},
                )
            )
            copies[-1].start()
    local = []
    for n, (target, lane) in enumerate(pieces):
        local.append(
            pltpu.make_async_copy(final.at[head, :, pl.ds(lane, DH)], target.at[:, here], lsem.at[n])
        )
        local[-1].start()
    for copy in local + copies:
        copy.wait()
    partner.wait_send()
    for copy in started.values():
        copy.wait_send()


def scatter_all(index, table, own):
    count = len(SCATTER_SENDS)
    return pl.pallas_call(
        scatter_kernel,
        out_shape=(jax.ShapeDtypeStruct((BLOCK, KVH * DH), BF16),) * 2,
        in_specs=[
            pl.BlockSpec(memory_space=pltpu.SMEM),
            pl.BlockSpec(memory_space=pltpu.VMEM),
            pl.BlockSpec(memory_space=pltpu.VMEM),
        ],
        out_specs=(pl.BlockSpec(memory_space=pl.ANY),) * 2,
        scratch_shapes=[
            pltpu.VMEM((2, RING, 2 * RING, BLOCK, PAIR), BF16),
            pltpu.VMEM((ROWS, BLOCK, PAIR), BF16),
            pltpu.VMEM((2, 2 * RING, BLOCK, PAIR), BF16),
            pltpu.VMEM((2, 2 * RING, BLOCK, PAIR), BF16),
            pltpu.VMEM((2, 2, BLOCK, PAIR), BF16),
            pltpu.VMEM((4, BLOCK, PAIR), BF16),
            pltpu.SemaphoreType.DMA((count,)),
            pltpu.SemaphoreType.DMA((count,)),
            pltpu.SemaphoreType.DMA((3, 2)),
            pltpu.SemaphoreType.DMA((3, 2)),
            pltpu.SemaphoreType.DMA((2,)),
            pltpu.SemaphoreType.DMA((2,)),
        ],
        compiler_params=pltpu.CompilerParams(collective_id=2, has_side_effects=True),
        name="scatter_terms",
    )(index, table, own)


def attention_kernel(spots, edges, same, queries, d_out, library, out, dq, table, own, kv, near, glob, sems):
    copies = [
        pltpu.make_async_copy(library.at[spots[e]], kv.at[e], sems.at[e]) for e in range(ROWS)
    ]
    for copy in copies:
        copy.start()
    near[...] = jnp.zeros_like(near)
    glob[...] = jnp.zeros_like(glob)
    table[NONE_ROW:] = jnp.zeros((ROWS - NONE_ROW, BLOCK, PAIR), BF16)
    for copy in copies:
        copy.wait()
    factor = DH ** (-0.5)
    dims = lambda a, b: (((a,), (b,)), ((), ()))

    def dot(a, b, at, bt):
        return lax.dot_general(a, b, dims(at, bt), preferred_element_type=F32)

    @pl.loop(0, 4)
    def _(i):
        rows = pl.ds(pl.multiple_of(i * BLOCK, BLOCK), BLOCK)
        stack = lambda ref: jnp.concatenate(
            [ref[rows, h * DH : (h + 1) * DH] for h in range(HEADS)], axis=0
        )
        q, g = stack(queries), stack(d_out)
        pairs = jnp.concatenate(
            [
                kv[pl.ds(i, 3)].reshape(3 * BLOCK, PAIR),
                kv[6:8].reshape(2 * BLOCK, PAIR),
                kv[pl.ds(8 + i * RAND, RAND)].reshape(RAND * BLOCK, PAIR),
            ],
            axis=0,
        )
        k, v = pairs[:, :DH], pairs[:, DH:]
        scores = dot(k, q, 1, 1) * factor
        cut_first = jnp.logical_and(i == 0, edges[0] == 1)
        cut_last = jnp.logical_and(i == 3, edges[1] == 1)
        scores = jnp.concatenate(
            [
                jnp.where(cut_first, NEG_FILL, scores[:BLOCK]),
                scores[BLOCK : 2 * BLOCK],
                jnp.where(cut_last, NEG_FILL, scores[2 * BLOCK : 3 * BLOCK]),
                scores[3 * BLOCK :],
            ],
            axis=0,
        )
        peak = jnp.max(scores, axis=0, keepdims=True)
        weights = jnp.exp(scores - peak)
        probs = weights * (1.0 / jnp.sum(weights, axis=0, keepdims=True))
        probs16 = probs.astype(BF16)
        result = dot(v, probs16, 0, 0).astype(BF16)
        delta = jnp.sum(g.T.astype(F32) * result.astype(F32), axis=0, keepdims=True)
        dprobs = dot(v, g, 1, 1)
        dscores = (probs * (dprobs - delta)).astype(BF16)
        dquery = (dot(k, dscores, 0, 0) * factor).astype(BF16).T
        result = result.T
        for h in range(HEADS):
            out[rows, h * DH : (h + 1) * DH] = result[h * BLOCK : (h + 1) * BLOCK]
            dq[rows, h * DH : (h + 1) * DH] = dquery[h * BLOCK : (h + 1) * BLOCK]
        dkey = dot(dscores, q, 1, 0) * factor
        dvalue = dot(probs16, g, 1, 0)
        terms = jnp.concatenate([dkey, dvalue], axis=1)
        near[pl.ds(i, 3)] += terms[: 3 * BLOCK].reshape(3, BLOCK, PAIR)
        glob[...] += terms[3 * BLOCK : 5 * BLOCK].reshape(2, BLOCK, PAIR)
        table[pl.ds(i * RAND, RAND)] = terms[5 * BLOCK :].astype(BF16).reshape(RAND, BLOCK, PAIR)

    own[...] = near[1:5]
    rest = (
        near[0].astype(BF16).astype(F32),
        near[5].astype(BF16).astype(F32),
        glob[0],
        glob[1],
    )
    for a in range(4):
        total = rest[a]
        for b in range(4):
            if a != b:
                total += jnp.where(same[a, b] == 1, rest[b], 0.0)
        table[32 + a] = total.astype(BF16)


def attention(spots, edges, same, queries, d_out, library):
    smem = pl.BlockSpec(memory_space=pltpu.SMEM)
    vmem = pl.BlockSpec(memory_space=pltpu.VMEM)
    return pl.pallas_call(
        attention_kernel,
        out_shape=(
            jax.ShapeDtypeStruct(queries.shape, BF16),
            jax.ShapeDtypeStruct(queries.shape, BF16),
            jax.ShapeDtypeStruct((ROWS, BLOCK, PAIR), BF16),
            jax.ShapeDtypeStruct((4, BLOCK, PAIR), F32),
        ),
        in_specs=[smem, smem, smem, vmem, vmem, pl.BlockSpec(memory_space=pl.ANY)],
        out_specs=(vmem,) * 4,
        scratch_shapes=[
            pltpu.VMEM((ROWS, BLOCK, PAIR), BF16),
            pltpu.VMEM((6, BLOCK, PAIR), F32),
            pltpu.VMEM((2, BLOCK, PAIR), F32),
            pltpu.SemaphoreType.DMA((ROWS,)),
        ],
        compiler_params=pltpu.CompilerParams(vmem_limit_bytes=60 * 1024 * 1024),
        name="block_attention",
    )(spots, edges, same, queries, d_out, library)


def slot_of(d):
    d = d % RING
    return jnp.where(d == 0, 0, jnp.where(d <= 4, 2 * d - 1, 2 * (RING - d)))


def body(queries, keys, values, d_out, rand_blocks, glob_blocks):
    seq, head, z, y, core = place()
    library, partner_rand = gather_all(keys, values, rand_blocks)
    library = library.reshape(512, BLOCK, PAIR)
    seq_count = lax.axis_size("seq")

    first = seq * 4
    window = jnp.clip(first - 1 + jnp.arange(6, dtype=jnp.int32), 0, seq_count * 4 - 1)
    ids = jnp.concatenate([window, glob_blocks, rand_blocks.reshape(-1)])
    owner, inner = ids // 4, ids % 4
    dz = slot_of(z - owner // 16)
    dy = slot_of(y - (owner // 2) % RING)
    half = inner // 2
    other = (owner % 2 != core).astype(jnp.int32)
    major = jnp.where(half == 0, dz, dy)
    minor = jnp.where(half == 0, dy, dz)
    spots = (((other * 2 + half) * 8 + major) * 8 + minor) * 2 + inner % 2
    edges = jnp.stack([seq == 0, seq == seq_count - 1]).astype(jnp.int32)

    def entries(at):
        return jnp.concatenate([jnp.stack([at * 4 - 1, at * 4 + 4]), glob_blocks])

    mine = entries(seq)
    same = (mine[:, None] == mine[None, :]).astype(jnp.int32)
    out, dq, table, own = attention(spots, edges, same, queries, d_out, library)

    flat = jnp.arange(256, dtype=jnp.int32)
    half = flat // 128

    def offset(slot):
        return jnp.where(slot % 2 == 1, (slot + 1) // 2, -(slot // 2))

    far, near = offset((flat // 16) % 8), offset((flat // 2) % 8)
    oz = (z - jnp.where(half == 0, far, near)) % RING
    oy = (y - jnp.where(half == 0, near, far)) % RING
    block = (oz * 16 + oy * 2 + core) * 4 + half * 2 + flat % 2

    def lookup(ids, base):
        numbers = base + jnp.arange(ids.shape[0], dtype=jnp.int32)
        hits = jnp.where(block[None, :] == ids[:, None], numbers[:, None], NONE_ROW)
        return jnp.min(hits, axis=0)

    index = jnp.stack(
        [
            lookup(rand_blocks.reshape(-1), 0),
            lookup(mine, 32),
            lookup(partner_rand.reshape(-1), 0),
            lookup(entries(seq + 1 - 2 * core), 32),
        ]
    )
    dk, dv = scatter_all(index, table, own)
    return (out, dq, dk, dv)


def solution(mesh):
    in_specs = (
        P("seq", "head"),
        P(("seq", "head"), None),
        P(("seq", "head"), None),
        P("seq", "head"),
        P("seq", None),
        P(),
    )
    out_specs = (
        P("seq", "head"),
        P("seq", "head"),
        P(("seq", "head"), None),
        P(("seq", "head"), None),
    )
    return jax.shard_map(body, mesh=mesh, in_specs=in_specs, out_specs=out_specs, check_vma=False)
```

time: 674 us -> 165 us (0.24)
  the two profiles are of different devices: /device:TPU:1 before, /device:TPU:24 now
where the time goes in v1:
time: 165 us
  Pallas kernels  155 us (94%)
  local copies, waits for them, and re-layouts  4.46 us (3%)
  other arithmetic  4.16 us (3%)
    pallas_call x1, Pallas kernels, gather_all(): pl.pallas_call(gather_kernel, out_shape=(jax.ShapeDtypeStruct((2, 2, RING...  73.7 us
    pallas_call x1, Pallas kernels, scatter_all(): pl.pallas_call(scatter_kernel, out_shape=(jax.ShapeDtypeStruct((BLOCK, KV...  69.5 us
    pallas_call x1, Pallas kernels, attention(): pl.pallas_call(attention_kernel, out_shape=(jax.ShapeDtypeStruct(queries....  11.9 us

profile of v1, /device:TPU:24, one launch (start us, length us, event | category | flops | bytes accessed | tf_op | source)
XLA Modules:
  0.0 164.5 jit_solution(4327570605850803575)
XLA Ops:
  0.7 73.7 %gather_blocks.1 = (bf16[2,2,8,16,64,256]{5,4,3,2,1,0:T(8,128)(2,1)}, s32[4,8]{1,0:T(4,128)}) custom-call(bf16[64,512]{1,0:T(8,128)(2,1)} %keys.1, bf16[64,512]{1,0:T(8,128)(2,1)} %values.1, s32[4,8]{1,0:T(4,128)} %rand.1), custom_call_target="tpu_custom_call" | custom-call | tf_op jit(solution)/shard_map/gather_blocks/pallas_call | solution.py:242
  74.4 0.8 eq.142
  75.2 0.8 reshape.206
  75.9 0.1 select_reduce_fusion.1
  76.0 0.7 add_add_fusion.1
  76.8 0.1 select_reduce_fusion.3
  76.9 0.6 pad_add_fusion.index
  77.5 0.6 compare_convert_fusion.same
  78.1 1.3 fusion.11.spots
  79.5 0.6 add_convert_fusion.edges
  80.1 11.9 %block_attention.1 = (bf16[256,1024]{1,0:T(8,128)(2,1)}, bf16[256,1024]{1,0:T(8,128)(2,1)}, bf16[40,64,256]{2,1,0:T(8,128)(2,1)}, f32[4,64,256]{2,1,0:T(8,128)}) custom-call(s32[40]{0:T(128)} %fusion.11.spots, s32[2]{0:T(128)} %add_convert_fusion.edges, s32[4,4]{1,0:T(4,128)} %compare_convert_fusion.same, bf16[256,1024]{1,0:T(8,128)(2,1)} %queries.1, ...), custom_call_target="tpu_custom_call" | custom-call | tf_op jit(solution)/shard_map/block_attention/pallas_call | solution.py:485
  92.0 69.5 %scatter_terms.1 = (bf16[64,512]{1,0:T(8,128)(2,1)}, bf16[64,512]{1,0:T(8,128)(2,1)}) custom-call(s32[4,256]{1,0:T(4,128)} %pad_add_fusion.index, bf16[40,64,256]{2,1,0:T(8,128)(2,1)} %get-tuple-element.16.table, f32[4,64,256]{2,1,0:T(8,128)} %get-tuple-element.17.own), custom_call_target="tpu_custom_call" | custom-call | tf_op jit(solution)/shard_map/scatter_terms/pallas_call | solution.py:374
  161.6 1.5 copy.12
  163.0 1.5 copy.13
  (2 shorter events, 0.0 us)

commit v2 on v1

v2 whole, which is shorter than its diff:
```python
import jax
import jax.numpy as jnp
from jax import lax
from jax.experimental import pallas as pl
from jax.experimental.pallas import tpu as pltpu
from jax.sharding import PartitionSpec as P

DH = 128
KVH = 4
HEADS = 8
BLOCK = 64
RAND = 8
PAIR = 2 * DH
RING = 8
NEG_FILL = -1e30
BF16 = jnp.bfloat16
F32 = jnp.float32
MESH = pl.DeviceIdType.MESH

ORDER = (0, 1, -1, 2, -2, 3, -3, 4)
SLOT = {d: i for i, d in enumerate(ORDER)}
ROWS = (0, 3, -3, 1, -1, 2, -2, 4)
PATH = {1: 24, -1: 25, 2: 26, -2: 27}
CHUNKS = 28
INNER = ((1, 3), (3, 5), (5, 7), (7, 8))
LEAVES = (
    (1, 1, 7, ((0, 3), (7, 8))),
    (2, -1, 7, ((3, 5), (5, 7))),
    (1, -1, 5, INNER),
    (2, 1, 6, INNER),
    (0, 1, 3, INNER),
    (0, -1, 4, INNER),
)
SIDES = {("z", 1): 0, ("z", -1): 1, ("y", 1): 2, ("y", -1): 3}
CHUNK_US = 1.78
HALF_US = 0.05
HOP_US = 1.7
KV_ROWS = 40
TERMS = 36
NO_TERM = 34


def axis_of(half, major):
    return "zy"[half] if major else "yz"[half]


def ordered(tasks):
    arrival, free, result = {}, {}, []
    waiting = list(tasks)
    while waiting:
        best = None
        for task in waiting:
            if all(dep in arrival for dep in task[3]):
                ready = max([arrival[dep] for dep in task[3]], default=0.0)
                if best is None or ready < best[0]:
                    best = (ready, task)
        ready, task = best
        waiting.remove(task)
        name, link, time, deps = task
        end = max(ready, free.get(link, 0.0)) + time
        free[link] = end
        arrival[name] = end + HOP_US
        result.append(task)
    return result, max(arrival.values())


def far_sign(half, row):
    return 1 if (half + row) % 2 == 0 else -1


def gather_tasks():
    tasks = []
    for half in (0, 1):
        minor, major = axis_of(half, False), axis_of(half, True)
        whole, leaf = {}, {}
        for step in range(3):
            for sign in (1, -1):
                name = ("H", half, sign, step)
                deps = (("H", half, sign, step - 1),) if step else ()
                tasks.append((name, (major, sign), CHUNK_US, deps))
                if step < 2:
                    whole[PATH[sign * (step + 1)]] = name
                else:
                    whole[8 if sign > 0 else 16] = name
        for row in range(3):
            far = far_sign(half, row)
            for sign in (1, -1):
                for step in range(4 if sign == far else 3):
                    name = ("m", half, row, sign, step)
                    if step:
                        deps = (("m", half, row, sign, step - 1),)
                    else:
                        deps = (whole[8 * row],) if row else ()
                    tasks.append((name, (minor, sign), CHUNK_US, deps))
                    to = 7 if step == 3 else SLOT[sign * (step + 1)]
                    whole[8 * row + to] = name
        for row, sign, to, ranges in LEAVES:
            for lo, hi in ranges:
                name = ("L", half, row, sign, to, lo, hi)
                deps = tuple(whole[8 * row + s] for s in range(lo, hi) if row or s)
                tasks.append((name, (major, sign), CHUNK_US * (hi - lo) / 2, deps))
                for s in range(lo, hi):
                    leaf[to, s] = name
        copies = tuple(whole.values())
        for sign in (1, -1):
            tasks.append((("G", half, sign), (major, sign), CHUNK_US / 2, copies))
        for sign in (1, -1):
            tasks.append((("X", half, sign), "p", HALF_US, (("G", half, sign),)))
        for row in range(8):
            groups = ((0, 5), (5, 8)) if row < 7 else ((0, 3), (3, 7), (7, 8))
            for lo, hi in groups:
                deps = []
                for s in range(lo, hi):
                    if row < 3:
                        deps.append(whole.get(8 * row + s))
                    elif row < 7 and s == 0:
                        deps.append(whole[PATH[ROWS[row]]])
                    else:
                        deps.append(leaf[row, s])
                deps = tuple(dict.fromkeys(d for d in deps if d))
                tasks.append((("P", half, row, lo, hi), "p", HALF_US * (hi - lo), deps))
    return ordered(tasks)[0]


def children(row, slot):
    if row == 0:
        return [(3, 1), (4, -1)] if slot else []
    result = []
    if slot:
        result.append((5, -1) if row == 1 else (6, 1))
    if row == 1 and slot in (0, 1, 2, 7):
        result.append((7, 1))
    if row == 2 and slot in (3, 4, 5, 6):
        result.append((7, -1))
    return result


def scatter_tasks():
    tasks = []
    for half in (0, 1):
        major = axis_of(half, True)
        for sign in (1, -1):
            tasks.append((("G", half, sign), (major, sign), CHUNK_US / 2, ()))
    leaf = {}
    for row, sign, to, ranges in LEAVES:
        for lo, hi in reversed(ranges):
            for half in (0, 1):
                major = axis_of(half, True)
                name = ("L", half, to, sign, lo, hi)
                tasks.append((name, (major, -sign), CHUNK_US * (hi - lo) / 2, ()))
                for s in range(lo, hi):
                    leaf[half, to, s] = name
    for half in (0, 1):
        minor, major = axis_of(half, False), axis_of(half, True)
        extra = (("G", half, 1), ("G", half, -1))

        def leaves(row, slot):
            return tuple(leaf[half, to, slot] for to, _ in children(row, slot)) + extra

        for row in (1, 2, 0):
            for sign in (1, -1):
                top = 4 if sign == far_sign(half, row) else 3
                for step in range(top, 0, -1):
                    deps = leaves(row, 7 if step == 4 else SLOT[sign * step])
                    if step < top:
                        deps += (("m", half, row, sign, step + 1),)
                    tasks.append((("m", half, row, sign, step), (minor, -sign), CHUNK_US, deps))
        for sign in (1, -1):
            row = 1 if sign > 0 else 2
            for step in (3, 2, 1):
                if step == 3:
                    deps = leaves(row, 0) + (("m", half, row, 1, 1), ("m", half, row, -1, 1))
                else:
                    deps = (("H", half, sign, step + 1),)
                tasks.append((("H", half, sign, step), (major, -sign), CHUNK_US, deps))
        deps = tuple((k, half, s, 1) for k in "H" for s in (1, -1))
        deps += (("m", half, 0, 1, 1), ("m", half, 0, -1, 1))
        tasks.append((("F", half), ("f", half), 0.0, deps))
    return ordered(tasks)[0]


GATHER = gather_tasks()
SCATTER = scatter_tasks()
GATHER_SENDS = {task[0]: i for i, task in enumerate(GATHER)}
SCATTER_SENDS = {t[0]: i for i, t in enumerate(t for t in SCATTER if t[0][0] != "F")}


def place():
    seq = lax.axis_index("seq")
    head = lax.axis_index("head")
    return seq, head, seq // 16, (seq // 2) % RING, seq % 2


def neighbours(seq, head, z, y, core):
    up = lambda v: lax.rem(v + 1, RING)
    down = lambda v: lax.rem(v + RING - 1, RING)
    index = lambda zz, yy, cc: zz * 16 + yy * 2 + cc
    count = 2 * RING * RING
    peers = {}
    for name, cc in ((0, core), (1, 1 - core)):
        peers["z", 1, name] = index(up(z), y, cc)
        peers["z", -1, name] = index(down(z), y, cc)
        peers["y", 1, name] = index(z, up(y), cc)
        peers["y", -1, name] = index(z, down(y), cc)
    peers["p"] = index(z, y, 1 - core)
    peers["next"] = lax.rem(seq + 1, count)
    peers["last"] = lax.rem(seq + count - 1, count)
    return {k: {"seq": v, "head": head} for k, v in peers.items()}


def enter(peers, seq, head):
    barrier = pltpu.get_barrier_semaphore()
    everyone = list(peers.values())
    everyone += [{"seq": seq, "head": lax.rem(head + j, KVH)} for j in (1, 2, 3)]
    for peer in everyone:
        pl.semaphore_signal(barrier, inc=1, device_id=peer, device_id_type=MESH)
    pl.semaphore_wait(barrier, len(everyone))


def remote(src, dst, send, recv, peer):
    return pltpu.make_async_remote_copy(
        src_ref=src,
        dst_ref=dst,
        send_sem=send,
        recv_sem=recv,
        device_id=peer,
        device_id_type=MESH,
    )


def owner_of(half, z, y, core, far, near):
    dz, dy = (far, near) if half == 0 else (near, far)
    return lax.rem(z - dz + RING, RING) * 16 + lax.rem(y - dy + RING, RING) * 2 + core


def chunk_offsets(chunk):
    if chunk < 24:
        return ROWS[chunk // 8], ORDER[chunk % 8]
    return (1, -1, 2, -2)[chunk - 24], 0


def gather_kernel(
    keys, values, rand, want, glob, sel_out, near_out, cand_out, rand_out, wants,
    full0, full1, picked, staged, extra, scal, send, recv, xsend, xrecv, osend, orecv, lsem, csem,
):
    seq, head, z, y, core = place()
    peers = neighbours(seq, head, z, y, core)
    full = (full0, full1)
    enter(peers, seq, head)
    pieces = (keys, values)
    xcopies = []
    for j in (1, 2, 3):
        to = lax.rem(head + j, KVH)
        for n, source in enumerate(pieces):
            xcopies.append(
                remote(
                    source.at[:, pl.ds(pl.multiple_of(to * DH, DH), DH)],
                    full[n].at[0, head],
                    xsend.at[j - 1, n],
                    xrecv.at[j - 1, n],
                    {"seq": seq, "head": to},
                )
            )
            xcopies[-1].start()
    ocopies = [remote(want, wants.at[9], osend.at[0], orecv.at[0], peers["p"])]
    for (axis, sign), side in SIDES.items():
        back = SIDES[axis, -sign] * 2
        for r in (0, 1):
            i = len(ocopies)
            peer = peers[axis, sign, r]
            ocopies.append(remote(want, wants.at[back + r], osend.at[i], orecv.at[i], peer))
    ocopies.append(remote(rand, rand_out, osend.at[9], orecv.at[9], peers["p"]))
    for copy in ocopies:
        copy.start()
    local = [pltpu.make_async_copy(want, wants.at[8], lsem.at[0])]
    for n, source in enumerate(pieces):
        mine = source.at[:, pl.ds(pl.multiple_of(head * DH, DH), DH)]
        local.append(pltpu.make_async_copy(mine, full[n].at[0, head], lsem.at[1 + n]))
    for copy in local:
        copy.start()
    for copy in local:
        copy.wait()
    for copy in xcopies:
        copy.wait_recv()

    started = {}
    waited = set()
    tail = []

    def wait_for(deps):
        for dep in deps:
            if dep not in waited:
                waited.add(dep)
                started[dep].wait_recv()

    def finish_start():
        for copy in ocopies:
            copy.wait_recv()
        scalars = pltpu.make_async_copy(wants, scal, lsem.at[0])
        scalars.start()
        for half in (0, 1):
            i = 10 + 2 * half
            tail.append(remote(full[half].at[0, 3], near_out.at[half, 0], osend.at[i], orecv.at[i], peers["next"]))
            tail.append(
                remote(full[half].at[0, 0], near_out.at[half, 5], osend.at[i + 1], orecv.at[i + 1], peers["last"])
            )
            tail.append(
                pltpu.make_async_copy(full[half].at[0], near_out.at[half, pl.ds(1, 4)], lsem.at[1 + half])
            )
        for copy in tail:
            copy.start()
        scalars.wait()

    def pick(half, chunk, side):
        far, near = chunk_offsets(chunk)
        inner = scal[side, 0, owner_of(half, z, y, core, far, near)]
        block = full[half][chunk, 0]
        for b in (1, 2, 3):
            block = jnp.where(inner == b, full[half][chunk, b], block)
        return block

    ready = False
    locals_ = []
    for name, link, _, deps in GATHER:
        wait_for(deps)
        kind, half = name[:2]
        major = axis_of(half, True)
        if kind in "LP" and not ready:
            finish_start()
            ready = True
        i = GATHER_SENDS[name]
        peer = peers["p"] if link == "p" else peers[link[0], link[1], 0]
        extra_sends = []
        if kind == "H":
            _, _, sign, step = name
            src = full[half].at[PATH[sign * step] if step else 0]
            dst = full[half].at[PATH[sign * (step + 1)] if step < 2 else (8 if sign > 0 else 16)]
        elif kind == "m":
            _, _, row, sign, step = name
            src = full[half].at[8 * row + SLOT[sign * step]]
            dst = full[half].at[8 * row + (7 if step == 3 else SLOT[sign * (step + 1)])]
        elif kind == "L":
            _, _, row, sign, to, lo, hi = name
            side = SIDES[major, sign] * 2
            for s in range(lo, hi):
                for r in (0, 1):
                    staged[half, r, to, s] = pick(half, 8 * row + s, side + r)
            src = staged.at[half, :, to, pl.ds(lo, hi - lo)]
            dst = picked.at[half, :, to, pl.ds(lo, hi - lo)]
        elif kind == "P":
            _, _, row, lo, hi = name
            for s in range(lo, hi):
                chunk = 8 * row + s if row < 3 else PATH[ROWS[row]] if row < 7 and s == 0 else None
                if chunk is not None:
                    for r in (0, 1):
                        picked[half, r, row, s] = pick(half, chunk, 8 + r)
            span = pl.ds(lo, hi - lo)
            src = picked.at[half, 1, row, span]
            dst = sel_out.at[1, half, row, span]
            keep = pltpu.make_async_copy(
                picked.at[half, 0, row, span], sel_out.at[0, half, row, span], csem.at[len(locals_)]
            )
            keep.start()
            locals_.append(keep)
        elif kind == "G":
            sign = name[2]
            if sign > 0:
                for k in (0, 1):
                    extra[half, k] = full[half][glob[half, k] // 4, glob[half, k] % 4]
                keep = pltpu.make_async_copy(extra.at[half], cand_out.at[0, half, 0], csem.at[len(locals_)])
                keep.start()
                locals_.append(keep)
                j = 14 + half
                tail.append(
                    remote(extra.at[half], cand_out.at[1, half, 0], osend.at[j], orecv.at[j], peers["p"])
                )
                tail[-1].start()
            src = extra.at[half]
            dst = cand_out.at[0, half, 2 if sign > 0 else 1]
        else:
            sign = name[2]
            at = 2 if sign > 0 else 1
            src = cand_out.at[0, half, at]
            dst = cand_out.at[1, half, at]
        copy = remote(src, dst, send.at[i], recv.at[i], peer)
        copy.start()
        started[name] = copy
    wait_for(started)
    for copy in xcopies + ocopies + list(started.values()):
        copy.wait_send()
    for copy in tail + locals_:
        copy.wait()


def gather_all(keys, values, rand, want, glob):
    count = len(GATHER)
    keeps = 2 + sum(task[0][0] == "P" for task in GATHER)
    hbm = pl.BlockSpec(memory_space=pl.ANY)
    vmem = pl.BlockSpec(memory_space=pltpu.VMEM)
    smem = pl.BlockSpec(memory_space=pltpu.SMEM)
    return pl.pallas_call(
        gather_kernel,
        out_shape=(
            jax.ShapeDtypeStruct((2, 2, 8, 8, BLOCK, DH), BF16),
            jax.ShapeDtypeStruct((2, 6, BLOCK, DH), BF16),
            jax.ShapeDtypeStruct((2, 2, 3, 2, BLOCK, DH), BF16),
            jax.ShapeDtypeStruct(rand.shape, jnp.int32),
            jax.ShapeDtypeStruct((10,) + want.shape, jnp.int32),
        ),
        in_specs=[vmem] * 4 + [smem],
        out_specs=(hbm, hbm, hbm, vmem, vmem),
        scratch_shapes=[
            pltpu.VMEM((CHUNKS, 4, BLOCK, DH), BF16),
            pltpu.VMEM((CHUNKS, 4, BLOCK, DH), BF16),
            pltpu.VMEM((2, 2, 8, 8, BLOCK, DH), BF16),
            pltpu.VMEM((2, 2, 8, 8, BLOCK, DH), BF16),
            pltpu.VMEM((2, 2, BLOCK, DH), BF16),
            pltpu.SMEM((10,) + want.shape, jnp.int32),
            pltpu.SemaphoreType.DMA((count,)),
            pltpu.SemaphoreType.DMA((count,)),
            pltpu.SemaphoreType.DMA((3, 2)),
            pltpu.SemaphoreType.DMA((3, 2)),
            pltpu.SemaphoreType.DMA((16,)),
            pltpu.SemaphoreType.DMA((16,)),
            pltpu.SemaphoreType.DMA((3,)),
            pltpu.SemaphoreType.DMA((keeps,)),
        ],
        compiler_params=pltpu.CompilerParams(collective_id=1, has_side_effects=True),
        name="gather_blocks",
    )(keys, values, rand, want, glob)


def scatter_kernel(
    index, leaf_index, wants, glob, table, own, halo, dk, dv,
    mirror, staged, landed, line, origin, path, stem, gsum, gin, extra, rim, final,
    send, recv, xsend, xrecv, psem, hsem, lsem,
):
    seq, head, z, y, core = place()
    peers = neighbours(seq, head, z, y, core)
    enter(peers, seq, head)
    first = [remote(table, mirror, psem.at[0], psem.at[1], peers["p"])]
    for half in (0, 1):
        i = 2 * half
        first.append(remote(halo.at[half, 0], rim.at[half, 1], hsem.at[0, i], hsem.at[1, i], peers["last"]))
        first.append(
            remote(halo.at[half, 1], rim.at[half, 0], hsem.at[0, i + 1], hsem.at[1, i + 1], peers["next"])
        )
    for copy in first:
        copy.start()
    first[0].wait_recv()
    for half in (0, 1):
        for k in (0, 1):
            gsum[half, k] = (table[half, 32 + k].astype(F32) + mirror[half, 32 + k].astype(F32)).astype(BF16)

    started = {}
    waited = set()
    ready = set()

    def block_sum(half, chunk, sides, b):
        far, near = chunk_offsets(chunk)
        owner = owner_of(half, z, y, core, far, near)
        spot = (half * CHUNKS + chunk) * 4 + b
        total = table[half, index[0, spot]].astype(F32) + mirror[half, index[1, spot]].astype(F32)
        kind = sum(1 if sign > 0 else 2 for _, sign in sides)
        number = owner * 4 + b
        total += jnp.where(
            number == glob[0],
            extra[half, kind, 0],
            jnp.where(number == glob[1], extra[half, kind, 1], 0.0),
        )
        major = axis_of(half, True)
        for to, sign in sides:
            for r in (0, 1):
                inner = wants[SIDES[major, sign] * 2 + r, 0, owner]
                term = landed[half, r, to, chunk % 8].astype(F32)
                total += jnp.where(inner == b, term, 0.0)
        return total

    for name, link, _, deps in SCATTER:
        for dep in deps:
            if dep not in waited:
                waited.add(dep)
                started[dep].wait_recv()
        kind, half = name[:2]
        if kind in "mHF" and half not in ready:
            ready.add(half)
            for k in (0, 1):
                alone = table[half, 32 + k].astype(F32) + mirror[half, 32 + k].astype(F32)
                up, down = gin[half, 0, k].astype(F32), gin[half, 1, k].astype(F32)
                extra[half, 0, k] = alone
                extra[half, 1, k] = alone + up
                extra[half, 2, k] = alone + down
                extra[half, 3, k] = alone + up + down
        if kind == "F":
            for copy in first[1 + 2 * half : 3 + 2 * half]:
                copy.wait_recv()

            for b in range(4):
                total = block_sum(half, 0, [], b) + own[half, b]
                total += line[half, 0, 0, b].astype(F32) + origin[half, 0, b].astype(F32)
                total += stem[half, 0, b].astype(F32) + stem[half, 1, b].astype(F32)
                if b in (0, 3):
                    total += rim[half, b // 3].astype(F32)
                final[half, b] = total.astype(BF16)
            continue
        if kind == "G":
            src, dst = gsum.at[half], gin.at[half, 1 if name[2] > 0 else 0]
        elif kind == "L":
            _, _, to, sign, lo, hi = name
            for s in range(lo, hi):
                for r, terms in ((0, table), (1, mirror)):
                    staged[half, r, to, s] = terms[half, leaf_index[r, (half * 8 + to) * 8 + s]]
            span = pl.ds(lo, hi - lo)
            src, dst = staged.at[half, :, to, span], landed.at[half, :, to, span]
        elif kind == "m":
            _, _, row, sign, step = name
            slot = 7 if step == 4 else SLOT[sign * step]
            arrived = any(dep[0] == "m" for dep in deps)
            sides = children(row, slot)

            @pl.loop(0, 4)
            def _(b):
                total = block_sum(half, 8 * row + slot, sides, b)
                if arrived:
                    total += line[half, row, slot, b].astype(F32)
                line[half, row, slot, b] = total.astype(BF16)

            src = line.at[half, row, slot]
            if step > 1:
                dst = line.at[half, row, SLOT[sign * (step - 1)]]
            else:
                dst = line.at[half, row, 0] if sign > 0 else origin.at[half, row]
        else:
            _, _, sign, step = name
            if step == 3:
                row = 1 if sign > 0 else 2
                sides = children(row, 0)

                @pl.loop(0, 4)
                def _(b):
                    total = block_sum(half, 8 * row, sides, b)
                    total += line[half, row, 0, b].astype(F32) + origin[half, row, b].astype(F32)
                    line[half, row, 0, b] = total.astype(BF16)

                src = line.at[half, row, 0]
            else:
                chunk = PATH[sign * step]

                @pl.loop(0, 4)
                def _(b):
                    total = block_sum(half, chunk, [], b) + path[half, chunk - 24, b].astype(F32)
                    path[half, chunk - 24, b] = total.astype(BF16)

                src = path.at[half, chunk - 24]
            if step > 1:
                dst = path.at[half, PATH[sign * (step - 1)] - 24]
            else:
                dst = stem.at[half, 0 if sign > 0 else 1]
        i = SCATTER_SENDS[name]
        copy = remote(src, dst, send.at[i], recv.at[i], peers[link[0], link[1], 0])
        copy.start()
        started[name] = copy

    here = pl.ds(pl.multiple_of(head * DH, DH), DH)
    copies = []
    for j in (1, 2, 3):
        to = lax.rem(head + j, KVH)
        for n, target in enumerate((dk, dv)):
            copies.append(
                remote(
                    final.at[n, to],
                    target.at[:, here],
                    xsend.at[j - 1, n],
                    xrecv.at[j - 1, n],
                    {"seq": seq, "head": to},
                )
            )
            copies[-1].start()
    for n, target in enumerate((dk, dv)):
        copies.append(pltpu.make_async_copy(final.at[n, head], target.at[:, here], lsem.at[n]))
        copies[-1].start()
    for copy in copies:
        copy.wait()
    for copy in first + list(started.values()):
        copy.wait_send()


def scatter_all(index, leaf_index, wants, glob, table, own, halo):
    count = len(SCATTER_SENDS)
    vmem = pl.BlockSpec(memory_space=pltpu.VMEM)
    smem = pl.BlockSpec(memory_space=pltpu.SMEM)
    tile = (BLOCK, DH)
    return pl.pallas_call(
        scatter_kernel,
        out_shape=(jax.ShapeDtypeStruct((BLOCK, KVH * DH), BF16),) * 2,
        in_specs=[smem] * 4 + [vmem] * 3,
        out_specs=(pl.BlockSpec(memory_space=pl.ANY),) * 2,
        scratch_shapes=[
            pltpu.VMEM((2, TERMS) + tile, BF16),
            pltpu.VMEM((2, 2, 8, 8) + tile, BF16),
            pltpu.VMEM((2, 2, 8, 8) + tile, BF16),
            pltpu.VMEM((2, 3, 8, 4) + tile, BF16),
            pltpu.VMEM((2, 3, 4) + tile, BF16),
            pltpu.VMEM((2, 4, 4) + tile, BF16),
            pltpu.VMEM((2, 2, 4) + tile, BF16),
            pltpu.VMEM((2, 2) + tile, BF16),
            pltpu.VMEM((2, 2, 2) + tile, BF16),
            pltpu.VMEM((2, 4, 2) + tile, F32),
            pltpu.VMEM((2, 2) + tile, BF16),
            pltpu.VMEM((2, 4) + tile, BF16),
            pltpu.SemaphoreType.DMA((count,)),
            pltpu.SemaphoreType.DMA((count,)),
            pltpu.SemaphoreType.DMA((3, 2)),
            pltpu.SemaphoreType.DMA((3, 2)),
            pltpu.SemaphoreType.DMA((2,)),
            pltpu.SemaphoreType.DMA((2, 4)),
            pltpu.SemaphoreType.DMA((2,)),
        ],
        compiler_params=pltpu.CompilerParams(collective_id=2, has_side_effects=True),
        name="scatter_terms",
    )(index, leaf_index, wants, glob, table, own, halo)


def attention_kernel(
    spots, edges, same, queries, d_out, selected, nearby, candidates,
    out, dq, table, own, halo, kv, near, glob, sems, gsems,
):
    copies = [pltpu.make_async_copy(nearby.at[n], kv.at[n, pl.ds(0, 6)], gsems.at[n]) for n in (0, 1)]
    for n in (0, 1):
        for k in (0, 1):
            copies.append(
                pltpu.make_async_copy(candidates.at[spots[n, k]], kv.at[n, 6 + k], gsems.at[2 + 2 * n + k])
            )
    for copy in copies:
        copy.start()

    def fetch(e, n):
        return pltpu.make_async_copy(selected.at[spots[n, 2 + e]], kv.at[n, 8 + e], sems.at[n, e])

    for e in range(4 * RAND):
        for n in (0, 1):
            fetch(e, n).start()
    near[...] = jnp.zeros_like(near)
    glob[...] = jnp.zeros_like(glob)
    for n in (0, 1):
        table[n, NO_TERM:] = jnp.zeros((TERMS - NO_TERM, BLOCK, DH), BF16)
    for copy in copies:
        copy.wait()
    for e in range(4 * RAND):
        for n in (0, 1):
            fetch(e, n).wait()
    factor = DH ** (-0.5)
    dims = lambda a, b: (((a,), (b,)), ((), ()))

    def dot(a, b, at, bt):
        return lax.dot_general(a, b, dims(at, bt), preferred_element_type=F32)

    @pl.loop(0, 4)
    def _(i):
        rows = pl.ds(pl.multiple_of(i * BLOCK, BLOCK), BLOCK)
        stack = lambda ref: jnp.concatenate(
            [ref[rows, h * DH : (h + 1) * DH] for h in range(HEADS)], axis=0
        )
        q, g = stack(queries), stack(d_out)

        def listed(n):
            return jnp.concatenate(
                [
                    kv[n, pl.ds(i, 3)].reshape(3 * BLOCK, DH),
                    kv[n, 6:8].reshape(2 * BLOCK, DH),
                    kv[n, pl.ds(8 + i * RAND, RAND)].reshape(RAND * BLOCK, DH),
                ],
                axis=0,
            )

        k, v = listed(0), listed(1)
        scores = dot(k, q, 1, 1) * factor
        cut_first = jnp.logical_and(i == 0, edges[0] == 1)
        cut_last = jnp.logical_and(i == 3, edges[1] == 1)
        scores = jnp.concatenate(
            [
                jnp.where(cut_first, NEG_FILL, scores[:BLOCK]),
                scores[BLOCK : 2 * BLOCK],
                jnp.where(cut_last, NEG_FILL, scores[2 * BLOCK : 3 * BLOCK]),
                scores[3 * BLOCK :],
            ],
            axis=0,
        )
        peak = jnp.max(scores, axis=0, keepdims=True)
        weights = jnp.exp(scores - peak)
        probs = weights * (1.0 / jnp.sum(weights, axis=0, keepdims=True))
        probs16 = probs.astype(BF16)
        result = dot(v, probs16, 0, 0).astype(BF16)
        delta = jnp.sum(g.T.astype(F32) * result.astype(F32), axis=0, keepdims=True)
        dprobs = dot(v, g, 1, 1)
        dscores = (probs * (dprobs - delta)).astype(BF16)
        dquery = (dot(k, dscores, 0, 0) * factor).astype(BF16).T
        result = result.T
        for h in range(HEADS):
            out[rows, h * DH : (h + 1) * DH] = result[h * BLOCK : (h + 1) * BLOCK]
            dq[rows, h * DH : (h + 1) * DH] = dquery[h * BLOCK : (h + 1) * BLOCK]
        for n, terms in ((0, dot(dscores, q, 1, 0) * factor), (1, dot(probs16, g, 1, 0))):
            near[n, pl.ds(i, 3)] += terms[: 3 * BLOCK].reshape(3, BLOCK, DH)
            glob[n] += terms[3 * BLOCK : 5 * BLOCK].reshape(2, BLOCK, DH)
            table[n, pl.ds(i * RAND, RAND)] = terms[5 * BLOCK :].astype(BF16).reshape(RAND, BLOCK, DH)

    for n in (0, 1):
        own[n] = near[n, 1:5]
        halo[n, 0] = near[n, 0].astype(BF16)
        halo[n, 1] = near[n, 5].astype(BF16)
        for a in (0, 1):
            total = glob[n, a] + jnp.where(same[0] == 1, glob[n, 1 - a], 0.0)
            table[n, 32 + a] = total.astype(BF16)


def attention(spots, edges, same, queries, d_out, selected, nearby, candidates):
    smem = pl.BlockSpec(memory_space=pltpu.SMEM)
    vmem = pl.BlockSpec(memory_space=pltpu.VMEM)
    tile = (BLOCK, DH)
    return pl.pallas_call(
        attention_kernel,
        out_shape=(
            jax.ShapeDtypeStruct(queries.shape, BF16),
            jax.ShapeDtypeStruct(queries.shape, BF16),
            jax.ShapeDtypeStruct((2, TERMS) + tile, BF16),
            jax.ShapeDtypeStruct((2, 4) + tile, F32),
            jax.ShapeDtypeStruct((2, 2) + tile, BF16),
        ),
        in_specs=[smem] * 3 + [vmem] * 2 + [pl.BlockSpec(memory_space=pl.ANY)] * 3,
        out_specs=(vmem,) * 5,
        scratch_shapes=[
            pltpu.VMEM((2, KV_ROWS) + tile, BF16),
            pltpu.VMEM((2, 6) + tile, F32),
            pltpu.VMEM((2, 2) + tile, F32),
            pltpu.SemaphoreType.DMA((2, 4 * RAND)),
            pltpu.SemaphoreType.DMA((6,)),
        ],
        compiler_params=pltpu.CompilerParams(vmem_limit_bytes=60 * 1024 * 1024),
        name="block_attention",
    )(spots, edges, same, queries, d_out, selected, nearby, candidates)


def chosen(value, table):
    result = jnp.full_like(value, table[0])
    for i, entry in enumerate(table[1:], 1):
        result = jnp.where(value == i, entry, result)
    return result


SLOTS_MOD = [SLOT[d] if d <= 4 else SLOT[d - RING] for d in range(RING)]
ROWS_MOD = [ROWS.index(d) if d <= 4 else ROWS.index(d - RING) for d in range(RING)]


def relation(z, y, owner, half):
    dz = (z - owner // 16) % RING
    dy = (y - (owner // 2) % RING) % RING
    far = jnp.where(half == 0, dz, dy)
    near = jnp.where(half == 0, dy, dz)
    return chosen(far, ROWS_MOD), chosen(near, SLOTS_MOD)


def body(queries, keys, values, d_out, rand_blocks, glob_blocks):
    seq, head, z, y, core = place()
    seq_count = lax.axis_size("seq")
    ints = lambda n: jnp.arange(n, dtype=jnp.int32)
    rand = rand_blocks.reshape(-1)
    owners = ints(seq_count)
    hits = jnp.where(rand[:, None] // 4 == owners[None, :], rand[:, None] % 4, 0)
    want = jnp.max(hits, axis=0)[None, :]

    halves = ints(2)[:, None]
    grow, gslot = relation(z, y, glob_blocks[None, :] // 4, halves)
    whole = jnp.where(grow < 3, grow * 8 + gslot, 24 + grow - 3)
    is_whole = (grow < 3) | ((gslot == 0) & (grow < 7))
    glob_at = jnp.where(is_whole, whole * 4 + glob_blocks[None, :] % 4, 0)
    selected, nearby, candidates, partner_rand, wants = gather_all(keys, values, rand_blocks, want, glob_at)

    away = (glob_blocks // 4 % 2 != core).astype(jnp.int32)[None, :]
    late = (gslot >= 3) & (gslot < 7)
    parent = chosen(grow, [0, 0, 0, 2, 1, 1, 2, 2])
    parent = jnp.where((grow == 7) & late, 1, parent)
    parent = jnp.where(is_whole, 0, parent)
    glob_spots = ((away * 2 + halves) * 3 + parent) * 2 + ints(2)[None, :]
    row, slot = relation(z, y, rand[None, :] // 4, halves)
    away = (rand // 4 % 2 != core).astype(jnp.int32)[None, :]
    rand_spots = ((away * 2 + halves) * 8 + row) * 8 + slot
    spots = jnp.concatenate([glob_spots, rand_spots], axis=1)
    edges = jnp.stack([seq == 0, seq == seq_count - 1]).astype(jnp.int32)
    same = (glob_blocks[:1] == glob_blocks[1:]).astype(jnp.int32)
    out, dq, table, own, halo = attention(
        spots,
        edges,
        same,
        queries,
        d_out,
        selected.reshape(256, BLOCK, DH),
        nearby,
        candidates.reshape(24, BLOCK, DH),
    )

    def owner_at(half, far, near):
        oz = (z - jnp.where(half == 0, far, near)) % RING
        oy = (y - jnp.where(half == 0, near, far)) % RING
        return oz * 16 + oy * 2 + core

    def lookup(ids, targets):
        numbers = ints(32)
        match = jnp.where(targets[None, :] == ids[:, None], numbers[:, None], NO_TERM)
        return jnp.min(match, axis=0)

    flat = ints(2 * CHUNKS * 4)
    half, chunk = flat // (CHUNKS * 4), flat // 4 % CHUNKS
    far = jnp.where(chunk < 24, chosen(chunk // 8, ROWS[:3]), chosen(chunk - 24, (1, -1, 2, -2)))
    near = jnp.where(chunk < 24, chosen(chunk % 8, ORDER), 0)
    block = owner_at(half, far, near) * 4 + flat % 4
    theirs = partner_rand.reshape(-1)
    index = jnp.stack([lookup(rand, block), lookup(theirs, block)])
    flat = ints(128)
    owner = owner_at(flat // 64, chosen(flat // 8 % 8, ROWS), chosen(flat % 8, ORDER))
    leaf_index = jnp.stack([lookup(rand // 4, owner), lookup(theirs // 4, owner)])
    dk, dv = scatter_all(index, leaf_index, wants, glob_blocks, table, own, halo)
    return (out, dq, dk, dv)


def solution(mesh):
    in_specs = (
        P("seq", "head"),
        P(("seq", "head"), None),
        P(("seq", "head"), None),
        P("seq", "head"),
        P("seq", None),
        P(),
    )
    out_specs = (
        P("seq", "head"),
        P("seq", "head"),
        P(("seq", "head"), None),
        P(("seq", "head"), None),
    )
    return jax.shard_map(body, mesh=mesh, in_specs=in_specs, out_specs=out_specs, check_vma=False)
```

time: 165 us -> 147 us (0.89)
  Pallas kernels: 155 us -> 134 us
    pallas_call x1, Pallas kernels: 69.5 us -> 57.2 us  [scatter_all(): pl.pallas_call(scatter_kernel, out_shape=(jax.ShapeDtypeStruct((BLOCK, KV...]
    pallas_call x1, Pallas kernels: 73.7 us -> 64.3 us  [gather_all(): pl.pallas_call(gather_kernel, out_shape=(jax.ShapeDtypeStruct((2, 2, 8, 8...]
where the time goes in v2:
time: 147 us; the launch traced here: 146 us
  Pallas kernels  134 us (91%)
  local copies, waits for them, and re-layouts  5.78 us (4%)
  other arithmetic  4.73 us (3%)
  between operations  2.03 us (1%)
    pallas_call x1, Pallas kernels, gather_all(): pl.pallas_call(gather_kernel, out_shape=(jax.ShapeDtypeStruct((2, 2, 8, 8...  64.3 us
    pallas_call x1, Pallas kernels, scatter_all(): pl.pallas_call(scatter_kernel, out_shape=(jax.ShapeDtypeStruct((BLOCK, KV...  57.2 us
    pallas_call x1, Pallas kernels, attention(): pl.pallas_call(attention_kernel, out_shape=(jax.ShapeDtypeStruct(queries....  12.2 us
    unnamed x2, local copies, waits for them, and re-layouts  2.95 us

profile of v2, /device:TPU:24, one launch (start us, length us, event | category | flops | bytes accessed | tf_op | source)
XLA Modules:
  0.0 146.2 jit_solution(15389374956104935148)
XLA Ops:
  0.7 0.8 reshape.656
  1.5 0.6 select_reduce_fusion.3
  2.1 0.7 and_select_fusion.25
  2.8 0.6 add_select_fusion
  3.5 64.3 %gather_blocks.1 = (bf16[2,2,8,8,64,128]{5,4,3,2,1,0:T(8,128)(2,1)}, bf16[2,6,64,128]{3,2,1,0:T(8,128)(2,1)}, bf16[2,2,3,2,64,128]{5,4,3,2,1,0:T(8,128)(2,1)}, s32[4,8]{1,0:T(4,128)}, s32[10,1,128]{2,1,0:T(1,128)}) custom-call(bf16[64,512]{1,0:T(8,128)(2,1)} %keys.1, bf16[64,512]{1,0:T(8,128)(2,1)} %values.1, s32[4,8]{1,0:T(4,128)} %rand.1, ...), custom_call_target="tpu_custom_call" | custom-call | tf_op jit(solution)/shard_map/gather_blocks/pallas_call | solution.py:401
  67.8 0.8 eq.541
  68.6 0.1 select_reduce_fusion.1
  68.7 0.6 pad_add_fusion.index
  69.3 0.1 fusion.31
  69.4 0.7 pad_add_fusion.1.spots
  70.0 0.6 add_convert_fusion.edges
  70.6 1.3 fusion.64
  73.3 12.2 %block_attention.1 = (bf16[256,1024]{1,0:T(8,128)(2,1)}, bf16[256,1024]{1,0:T(8,128)(2,1)}, bf16[2,36,64,128]{3,2,1,0:T(8,128)(2,1)}, f32[2,4,64,128]{3,2,1,0:T(8,128)}, bf16[2,2,64,128]{3,2,1,0:T(8,128)(2,1)}) custom-call(s32[2,34]{1,0:T(2,128)} %pad_add_fusion.1.spots, s32[2]{0:T(128)} %add_convert_fusion.edges, s32[1]{0:T(128)S(6)} %convert_element_type.10.same, ...), custom_call_target="tpu_custom_call" | custom-call | tf_op jit(solution)/shard_map/block_attention/pallas_call | solution.py:720
  85.4 0.1 select_reduce_fusion.2
  85.5 0.5 pad_add_fusion.2.leaf_index
  86.1 57.2 %scatter_terms.1 = (bf16[64,512]{1,0:T(8,128)(2,1)}, bf16[64,512]{1,0:T(8,128)(2,1)}) custom-call(s32[2,224]{1,0:T(2,128)} %pad_add_fusion.index, s32[2,128]{1,0:T(2,128)} %pad_add_fusion.2.leaf_index, s32[10,1,128]{2,1,0:T(1,128)} %get-tuple-element.22.wants, s32[2]{0:T(128)} %glob.1, bf16[2,36,64,128]{3,2,1,0:T(8,128)(2,1)} %get-tuple-element.23.table, ...), custom_call_target="tpu_custom_call" | custom-call | tf_op jit(solution)/shard_map/scatter_terms/pallas_call | solution.py:593
  143.2 1.5 %copy.12 = bf16[64,512]{1,0:T(8,128)(2,1)} copy(bf16[64,512]{1,0:T(8,128)(2,1)} %get-tuple-element.52) | data formatting | bytes 131072
  144.7 1.5 %copy.13 = bf16[64,512]{1,0:T(8,128)(2,1)} copy(bf16[64,512]{1,0:T(8,128)(2,1)} %get-tuple-element.53) | data formatting | bytes 131072
  (7 shorter events, 0.1 us)

commit v3 on v2

--- a/solution.py
+++ b/solution.py
@@ -34,10 +34,12 @@
 SIDES = {("z", 1): 0, ("z", -1): 1, ("y", 1): 2, ("y", -1): 3}
 CHUNK_US = 1.78
 HALF_US = 0.05
-HOP_US = 1.7
+HOP_US = 2.8
+TABLE_US = 3.0
 KV_ROWS = 40
 TERMS = 36
 NO_TERM = 34
+WANT = (1, 2 * RING * RING)
 
 
 def axis_of(half, major):
@@ -45,6 +47,18 @@
 
 
 def ordered(tasks):
+    followers = {}
+    for task in tasks:
+        for dep in task[3]:
+            followers.setdefault(dep, []).append(task)
+    left = {}
+
+    def remaining(task):
+        if task[0] not in left:
+            after = max((remaining(t) for t in followers.get(task[0], ())), default=0.0)
+            left[task[0]] = task[2] + HOP_US + after
+        return left[task[0]]
+
     arrival, free, result = {}, {}, []
     waiting = list(tasks)
     while waiting:
@@ -52,14 +66,14 @@
         for task in waiting:
             if all(dep in arrival for dep in task[3]):
                 ready = max([arrival[dep] for dep in task[3]], default=0.0)
-                if best is None or ready < best[0]:
-                    best = (ready, task)
-        ready, task = best
+                key = (max(ready, free.get(task[1], 0.0)), -remaining(task))
+                if best is None or key < best[0]:
+                    best = (key, task)
+        (start, _), task = best
         waiting.remove(task)
         name, link, time, deps = task
-        end = max(ready, free.get(link, 0.0)) + time
-        free[link] = end
-        arrival[name] = end + HOP_US
+        free[link] = start + time
+        arrival[name] = start + time + HOP_US
         result.append(task)
     return result, max(arrival.values())
 
@@ -119,7 +133,15 @@
                         deps.append(leaf[row, s])
                 deps = tuple(dict.fromkeys(d for d in deps if d))
                 tasks.append((("P", half, row, lo, hi), "p", HALF_US * (hi - lo), deps))
-    return ordered(tasks)[0]
+    late = [task for task in ordered(tasks)[0] if task[0][0] in "PX"]
+    result, seen = [], set()
+    for task in ordered([task for task in tasks if task[0][0] not in "PX"])[0]:
+        result.append(task)
+        seen.update(task[3])
+        for other in [t for t in late if set(t[3]) <= seen]:
+            late.remove(other)
+            result.append(other)
+    return result + late
 
 
 def children(row, slot):
@@ -136,26 +158,28 @@
 
 
 def scatter_tasks():
-    tasks = []
+    tasks = [(("T", 0), "p", TABLE_US, ())]
     for half in (0, 1):
         major = axis_of(half, True)
         for sign in (1, -1):
-            tasks.append((("G", half, sign), (major, sign), CHUNK_US / 2, ()))
+            tasks.append((("G", half, sign), (major, sign), CHUNK_US / 2, (("T", 0),)))
     leaf = {}
     for row, sign, to, ranges in LEAVES:
         for lo, hi in reversed(ranges):
             for half in (0, 1):
                 major = axis_of(half, True)
-                name = ("L", half, to, sign, lo, hi)
-                tasks.append((name, (major, -sign), CHUNK_US * (hi - lo) / 2, ()))
-                for s in range(lo, hi):
-                    leaf[half, to, s] = name
+                for r in (0, 1):
+                    name = ("L", half, to, sign, lo, hi, r)
+                    deps = (("T", 0),) if r else ()
+                    tasks.append((name, (major, -sign), CHUNK_US * (hi - lo) / 4, deps))
+                    for s in range(lo, hi):
+                        leaf[half, to, s, r] = name
     for half in (0, 1):
         minor, major = axis_of(half, False), axis_of(half, True)
         extra = (("G", half, 1), ("G", half, -1))
 
         def leaves(row, slot):
-            return tuple(leaf[half, to, slot] for to, _ in children(row, slot)) + extra
+            return tuple(leaf[half, to, slot, r] for to, _ in children(row, slot) for r in (0, 1)) + extra
 
         for row in (1, 2, 0):
             for sign in (1, -1):
@@ -239,13 +263,41 @@
     return (1, -1, 2, -2)[chunk - 24], 0
 
 
+def chosen(value, table):
+    result = table[0]
+    for i, entry in enumerate(table[1:], 1):
+        result = jnp.where(value == i, entry, result)
+    return result
+
+
+SLOTS_MOD = [SLOT[d] if d <= 4 else SLOT[d - RING] for d in range(RING)]
+ROWS_MOD = [ROWS.index(d) if d <= 4 else ROWS.index(d - RING) for d in range(RING)]
+PARENT = [0, 0, 0, 2, 1, 1, 2, 2]
+
+
+def relation(z, y, owner, half):
+    dz = (z + RING - owner // 16) % RING
+    dy = (y + RING - (owner // 2) % RING) % RING
+    far, near = (dz, dy) if half == 0 else (dy, dz)
+    return chosen(far, ROWS_MOD), chosen(near, SLOTS_MOD)
+
+
 def gather_kernel(
-    keys, values, rand, want, glob, sel_out, near_out, cand_out, rand_out, wants,
+    keys, values, rand, glob, sel_out, near_out, cand_out, wants, want,
     full0, full1, picked, staged, extra, scal, send, recv, xsend, xrecv, osend, orecv, lsem, csem,
 ):
     seq, head, z, y, core = place()
     peers = neighbours(seq, head, z, y, core)
     full = (full0, full1)
+    lane = lax.broadcasted_iota(jnp.int32, (1, 2 * RING * RING), 1)
+    named = jnp.full_like(lane, 4 * NO_TERM)
+    for e in range(4 * RAND):
+        block = rand[e // RAND, e % RAND]
+        named = jnp.where(lane == block // 4, 4 * e + block % 4, named)
+    want[...] = named
+    local = pltpu.make_async_copy(want, wants.at[8], lsem.at[0])
+    local.start()
+    local.wait()
     enter(peers, seq, head)
     pieces = (keys, values)
     xcopies = []
@@ -262,17 +314,16 @@
                 )
             )
             xcopies[-1].start()
-    ocopies = [remote(want, wants.at[9], osend.at[0], orecv.at[0], peers["p"])]
+    ocopies = [remote(wants.at[8], wants.at[9], osend.at[0], orecv.at[0], peers["p"])]
     for (axis, sign), side in SIDES.items():
         back = SIDES[axis, -sign] * 2
         for r in (0, 1):
             i = len(ocopies)
             peer = peers[axis, sign, r]
-            ocopies.append(remote(want, wants.at[back + r], osend.at[i], orecv.at[i], peer))
-    ocopies.append(remote(rand, rand_out, osend.at[9], orecv.at[9], peers["p"]))
+            ocopies.append(remote(wants.at[8], wants.at[back + r], osend.at[i], orecv.at[i], peer))
     for copy in ocopies:
         copy.start()
-    local = [pltpu.make_async_copy(want, wants.at[8], lsem.at[0])]
+    local = []
     for n, source in enumerate(pieces):
         mine = source.at[:, pl.ds(pl.multiple_of(head * DH, DH), DH)]
         local.append(pltpu.make_async_copy(mine, full[n].at[0, head], lsem.at[1 + n]))
@@ -313,13 +364,14 @@
 
     def pick(half, chunk, side):
         far, near = chunk_offsets(chunk)
-        inner = scal[side, 0, owner_of(half, z, y, core, far, near)]
+        inner = scal[side, 0, owner_of(half, z, y, core, far, near)] % 4
         block = full[half][chunk, 0]
         for b in (1, 2, 3):
             block = jnp.where(inner == b, full[half][chunk, b], block)
         return block
 
     ready = False
+    passed = set()
     locals_ = []
     for name, link, _, deps in GATHER:
         wait_for(deps)
@@ -364,9 +416,12 @@
             locals_.append(keep)
         elif kind == "G":
             sign = name[2]
-            if sign > 0:
+            if half not in passed:
+                passed.add(half)
                 for k in (0, 1):
-                    extra[half, k] = full[half][glob[half, k] // 4, glob[half, k] % 4]
+                    row, slot = relation(z, y, glob[k] // 4, half)
+                    chunk = jnp.where(row < 3, row * 8 + slot, jnp.where(row < 7, 21 + row, 0))
+                    extra[half, k] = full[half][chunk, glob[k] % 4]
                 keep = pltpu.make_async_copy(extra.at[half], cand_out.at[0, half, 0], csem.at[len(locals_)])
                 keep.start()
                 locals_.append(keep)
@@ -392,7 +447,7 @@
         copy.wait()
 
 
-def gather_all(keys, values, rand, want, glob):
+def gather_all(keys, values, rand, glob):
     count = len(GATHER)
     keeps = 2 + sum(task[0][0] == "P" for task in GATHER)
     hbm = pl.BlockSpec(memory_space=pl.ANY)
@@ -404,18 +459,18 @@
             jax.ShapeDtypeStruct((2, 2, 8, 8, BLOCK, DH), BF16),
             jax.ShapeDtypeStruct((2, 6, BLOCK, DH), BF16),
             jax.ShapeDtypeStruct((2, 2, 3, 2, BLOCK, DH), BF16),
-            jax.ShapeDtypeStruct(rand.shape, jnp.int32),
-            jax.ShapeDtypeStruct((10,) + want.shape, jnp.int32),
+            jax.ShapeDtypeStruct((10,) + WANT, jnp.int32),
         ),
-        in_specs=[vmem] * 4 + [smem],
-        out_specs=(hbm, hbm, hbm, vmem, vmem),
+        in_specs=[vmem] * 2 + [smem] * 2,
+        out_specs=(hbm, hbm, hbm, vmem),
         scratch_shapes=[
+            pltpu.VMEM(WANT, jnp.int32),
             pltpu.VMEM((CHUNKS, 4, BLOCK, DH), BF16),
             pltpu.VMEM((CHUNKS, 4, BLOCK, DH), BF16),
             pltpu.VMEM((2, 2, 8, 8, BLOCK, DH), BF16),
             pltpu.VMEM((2, 2, 8, 8, BLOCK, DH), BF16),
             pltpu.VMEM((2, 2, BLOCK, DH), BF16),
-            pltpu.SMEM((10,) + want.shape, jnp.int32),
+            pltpu.SMEM((10,) + WANT, jnp.int32),
             pltpu.SemaphoreType.DMA((count,)),
             pltpu.SemaphoreType.DMA((count,)),
             pltpu.SemaphoreType.DMA((3, 2)),
@@ -427,40 +482,35 @@
         ],
         compiler_params=pltpu.CompilerParams(collective_id=1, has_side_effects=True),
         name="gather_blocks",
-    )(keys, values, rand, want, glob)
+    )(keys, values, rand, glob)
 
 
 def scatter_kernel(
-    index, leaf_index, wants, glob, table, own, halo, dk, dv,
+    wants, glob, table, own, halo, dk, dv,
     mirror, staged, landed, line, origin, path, stem, gsum, gin, extra, rim, final,
-    send, recv, xsend, xrecv, psem, hsem, lsem,
+    send, recv, xsend, xrecv, hsem, lsem,
 ):
     seq, head, z, y, core = place()
     peers = neighbours(seq, head, z, y, core)
     enter(peers, seq, head)
-    first = [remote(table, mirror, psem.at[0], psem.at[1], peers["p"])]
+    first = []
     for half in (0, 1):
         i = 2 * half
         first.append(remote(halo.at[half, 0], rim.at[half, 1], hsem.at[0, i], hsem.at[1, i], peers["last"]))
         first.append(
             remote(halo.at[half, 1], rim.at[half, 0], hsem.at[0, i + 1], hsem.at[1, i + 1], peers["next"])
         )
-    for copy in first:
-        copy.start()
-    first[0].wait_recv()
-    for half in (0, 1):
-        for k in (0, 1):
-            gsum[half, k] = (table[half, 32 + k].astype(F32) + mirror[half, 32 + k].astype(F32)).astype(BF16)
-
     started = {}
     waited = set()
     ready = set()
+    passed = set()
 
     def block_sum(half, chunk, sides, b):
         far, near = chunk_offsets(chunk)
         owner = owner_of(half, z, y, core, far, near)
-        spot = (half * CHUNKS + chunk) * 4 + b
-        total = table[half, index[0, spot]].astype(F32) + mirror[half, index[1, spot]].astype(F32)
+        mine, theirs = wants[8, 0, owner], wants[9, 0, owner]
+        total = jnp.where(mine % 4 == b, table[half, mine // 4].astype(F32), 0.0)
+        total += jnp.where(theirs % 4 == b, mirror[half, theirs // 4].astype(F32), 0.0)
         kind = sum(1 if sign > 0 else 2 for _, sign in sides)
         number = owner * 4 + b
         total += jnp.where(
@@ -471,7 +521,7 @@
         major = axis_of(half, True)
         for to, sign in sides:
             for r in (0, 1):
-                inner = wants[SIDES[major, sign] * 2 + r, 0, owner]
+                inner = wants[SIDES[major, sign] * 2 + r, 0, owner] % 4
                 term = landed[half, r, to, chunk % 8].astype(F32)
                 total += jnp.where(inner == b, term, 0.0)
         return total
@@ -492,7 +542,7 @@
                 extra[half, 2, k] = alone + down
                 extra[half, 3, k] = alone + up + down
         if kind == "F":
-            for copy in first[1 + 2 * half : 3 + 2 * half]:
+            for copy in first[2 * half : 2 * half + 2]:
                 copy.wait_recv()
 
             for b in range(4):
@@ -503,15 +553,22 @@
                     total += rim[half, b // 3].astype(F32)
                 final[half, b] = total.astype(BF16)
             continue
-        if kind == "G":
+        if kind == "T":
+            src, dst = table, mirror
+        elif kind == "G":
+            if half not in passed:
+                passed.add(half)
+                for k in (0, 1):
+                    alone = table[half, 32 + k].astype(F32) + mirror[half, 32 + k].astype(F32)
+                    gsum[half, k] = alone.astype(BF16)
             src, dst = gsum.at[half], gin.at[half, 1 if name[2] > 0 else 0]
         elif kind == "L":
-            _, _, to, sign, lo, hi = name
+            _, _, to, sign, lo, hi, r = name
             for s in range(lo, hi):
-                for r, terms in ((0, table), (1, mirror)):
-                    staged[half, r, to, s] = terms[half, leaf_index[r, (half * 8 + to) * 8 + s]]
+                owner = owner_of(half, z, y, core, ROWS[to], ORDER[s])
+                staged[half, r, to, s] = (table, mirror)[r][half, wants[8 + r, 0, owner] // 4]
             span = pl.ds(lo, hi - lo)
-            src, dst = staged.at[half, :, to, span], landed.at[half, :, to, span]
+            src, dst = staged.at[half, r, to, span], landed.at[half, r, to, span]
         elif kind == "m":
             _, _, row, sign, step = name
             slot = 7 if step == 4 else SLOT[sign * step]
@@ -557,9 +614,13 @@
             else:
                 dst = stem.at[half, 0 if sign > 0 else 1]
         i = SCATTER_SENDS[name]
-        copy = remote(src, dst, send.at[i], recv.at[i], peers[link[0], link[1], 0])
+        peer = peers["p"] if link == "p" else peers[link[0], link[1], 0]
+        copy = remote(src, dst, send.at[i], recv.at[i], peer)
         copy.start()
         started[name] = copy
+        if kind == "T":
+            for copy in first:
+                copy.start()
 
     here = pl.ds(pl.multiple_of(head * DH, DH), DH)
     copies = []
@@ -585,7 +646,7 @@
         copy.wait_send()
 
 
-def scatter_all(index, leaf_index, wants, glob, table, own, halo):
+def scatter_all(wants, glob, table, own, halo):
     count = len(SCATTER_SENDS)
     vmem = pl.BlockSpec(memory_space=pltpu.VMEM)
     smem = pl.BlockSpec(memory_space=pltpu.SMEM)
@@ -593,7 +654,7 @@
     return pl.pallas_call(
         scatter_kernel,
         out_shape=(jax.ShapeDtypeStruct((BLOCK, KVH * DH), BF16),) * 2,
-        in_specs=[smem] * 4 + [vmem] * 3,
+        in_specs=[smem] * 2 + [vmem] * 3,
         out_specs=(pl.BlockSpec(memory_space=pl.ANY),) * 2,
         scratch_shapes=[
             pltpu.VMEM((2, TERMS) + tile, BF16),
@@ -612,43 +673,48 @@
             pltpu.SemaphoreType.DMA((count,)),
             pltpu.SemaphoreType.DMA((3, 2)),
             pltpu.SemaphoreType.DMA((3, 2)),
-            pltpu.SemaphoreType.DMA((2,)),
             pltpu.SemaphoreType.DMA((2, 4)),
             pltpu.SemaphoreType.DMA((2,)),
         ],
         compiler_params=pltpu.CompilerParams(collective_id=2, has_side_effects=True),
         name="scatter_terms",
-    )(index, leaf_index, wants, glob, table, own, halo)
+    )(wants, glob, table, own, halo)
 
 
 def attention_kernel(
-    spots, edges, same, queries, d_out, selected, nearby, candidates,
+    rand, ids, queries, d_out, selected, nearby, candidates,
     out, dq, table, own, halo, kv, near, glob, sems, gsems,
 ):
+    seq, _, z, y, core = place()
     copies = [pltpu.make_async_copy(nearby.at[n], kv.at[n, pl.ds(0, 6)], gsems.at[n]) for n in (0, 1)]
-    for n in (0, 1):
-        for k in (0, 1):
+    for e in range(4 * RAND):
+        owner = rand[e // RAND, e % RAND] // 4
+        away = (owner + core) % 2
+        for n in (0, 1):
+            row, slot = relation(z, y, owner, n)
+            spot = ((away * 2 + n) * 8 + row) * 8 + slot
+            copies.append(pltpu.make_async_copy(selected.at[spot], kv.at[n, 8 + e], sems.at[n, e]))
+    for k in (0, 1):
+        owner = ids[k] // 4
+        away = (owner + core) % 2
+        for n in (0, 1):
+            row, slot = relation(z, y, owner, n)
+            whole = (row < 3) | ((slot == 0) & (row < 7))
+            parent = chosen(row, PARENT)
+            parent = jnp.where((row == 7) & (slot >= 3) & (slot < 7), 1, parent)
+            parent = jnp.where(whole, 0, parent)
+            spot = ((away * 2 + n) * 3 + parent) * 2 + k
             copies.append(
-                pltpu.make_async_copy(candidates.at[spots[n, k]], kv.at[n, 6 + k], gsems.at[2 + 2 * n + k])
+                pltpu.make_async_copy(candidates.at[spot], kv.at[n, 6 + k], gsems.at[2 + 2 * n + k])
             )
     for copy in copies:
         copy.start()
-
-    def fetch(e, n):
-        return pltpu.make_async_copy(selected.at[spots[n, 2 + e]], kv.at[n, 8 + e], sems.at[n, e])
-
-    for e in range(4 * RAND):
-        for n in (0, 1):
-            fetch(e, n).start()
     near[...] = jnp.zeros_like(near)
     glob[...] = jnp.zeros_like(glob)
     for n in (0, 1):
         table[n, NO_TERM:] = jnp.zeros((TERMS - NO_TERM, BLOCK, DH), BF16)
     for copy in copies:
         copy.wait()
-    for e in range(4 * RAND):
-        for n in (0, 1):
-            fetch(e, n).wait()
     factor = DH ** (-0.5)
     dims = lambda a, b: (((a,), (b,)), ((), ()))
 
@@ -675,8 +741,8 @@
 
         k, v = listed(0), listed(1)
         scores = dot(k, q, 1, 1) * factor
-        cut_first = jnp.logical_and(i == 0, edges[0] == 1)
-        cut_last = jnp.logical_and(i == 3, edges[1] == 1)
+        cut_first = jnp.logical_and(i == 0, seq == 0)
+        cut_last = jnp.logical_and(i == 3, seq == lax.axis_size("seq") - 1)
         scores = jnp.concatenate(
             [
                 jnp.where(cut_first, NEG_FILL, scores[:BLOCK]),
@@ -709,11 +775,11 @@
         halo[n, 0] = near[n, 0].astype(BF16)
         halo[n, 1] = near[n, 5].astype(BF16)
         for a in (0, 1):
-            total = glob[n, a] + jnp.where(same[0] == 1, glob[n, 1 - a], 0.0)
+            total = glob[n, a] + jnp.where(ids[0] == ids[1], glob[n, 1 - a], 0.0)
             table[n, 32 + a] = total.astype(BF16)
 
 
-def attention(spots, edges, same, queries, d_out, selected, nearby, candidates):
+def attention(rand, ids, queries, d_out, selected, nearby, candidates):
     smem = pl.BlockSpec(memory_space=pltpu.SMEM)
     vmem = pl.BlockSpec(memory_space=pltpu.VMEM)
     tile = (BLOCK, DH)
@@ -726,7 +792,7 @@
             jax.ShapeDtypeStruct((2, 4) + tile, F32),
             jax.ShapeDtypeStruct((2, 2) + tile, BF16),
         ),
-        in_specs=[smem] * 3 + [vmem] * 2 + [pl.BlockSpec(memory_space=pl.ANY)] * 3,
+        in_specs=[smem] * 2 + [vmem] * 2 + [pl.BlockSpec(memory_space=pl.ANY)] * 3,
         out_specs=(vmem,) * 5,
         scratch_shapes=[
             pltpu.VMEM((2, KV_ROWS) + tile, BF16),
@@ -737,88 +803,29 @@
         ],
         compiler_params=pltpu.CompilerParams(vmem_limit_bytes=60 * 1024 * 1024),
         name="block_attention",
-    )(spots, edges, same, queries, d_out, selected, nearby, candidates)
-
-
-def chosen(value, table):
-    result = jnp.full_like(value, table[0])
-    for i, entry in enumerate(table[1:], 1):
-        result = jnp.where(value == i, entry, result)
-    return result
-
-
-SLOTS_MOD = [SLOT[d] if d <= 4 else SLOT[d - RING] for d in range(RING)]
-ROWS_MOD = [ROWS.index(d) if d <= 4 else ROWS.index(d - RING) for d in range(RING)]
-
-
-def relation(z, y, owner, half):
-    dz = (z - owner // 16) % RING
-    dy = (y - (owner // 2) % RING) % RING
-    far = jnp.where(half == 0, dz, dy)
-    near = jnp.where(half == 0, dy, dz)
-    return chosen(far, ROWS_MOD), chosen(near, SLOTS_MOD)
+    )(rand, ids, queries, d_out, selected, nearby, candidates)
+
+
+def copy_kernel(a, b, x, y):
+    x[...] = a[...]
+    y[...] = b[...]
 
 
 def body(queries, keys, values, d_out, rand_blocks, glob_blocks):
-    seq, head, z, y, core = place()
-    seq_count = lax.axis_size("seq")
-    ints = lambda n: jnp.arange(n, dtype=jnp.int32)
-    rand = rand_blocks.reshape(-1)
-    owners = ints(seq_count)
-    hits = jnp.where(rand[:, None] // 4 == owners[None, :], rand[:, None] % 4, 0)
-    want = jnp.max(hits, axis=0)[None, :]
-
-    halves = ints(2)[:, None]
-    grow, gslot = relation(z, y, glob_blocks[None, :] // 4, halves)
-    whole = jnp.where(grow < 3, grow * 8 + gslot, 24 + grow - 3)
-    is_whole = (grow < 3) | ((gslot == 0) & (grow < 7))
-    glob_at = jnp.where(is_whole, whole * 4 + glob_blocks[None, :] % 4, 0)
-    selected, nearby, candidates, partner_rand, wants = gather_all(keys, values, rand_blocks, want, glob_at)
-
-    away = (glob_blocks // 4 % 2 != core).astype(jnp.int32)[None, :]
-    late = (gslot >= 3) & (gslot < 7)
-    parent = chosen(grow, [0, 0, 0, 2, 1, 1, 2, 2])
-    parent = jnp.where((grow == 7) & late, 1, parent)
-    parent = jnp.where(is_whole, 0, parent)
-    glob_spots = ((away * 2 + halves) * 3 + parent) * 2 + ints(2)[None, :]
-    row, slot = relation(z, y, rand[None, :] // 4, halves)
-    away = (rand // 4 % 2 != core).astype(jnp.int32)[None, :]
-    rand_spots = ((away * 2 + halves) * 8 + row) * 8 + slot
-    spots = jnp.concatenate([glob_spots, rand_spots], axis=1)
-    edges = jnp.stack([seq == 0, seq == seq_count - 1]).astype(jnp.int32)
-    same = (glob_blocks[:1] == glob_blocks[1:]).astype(jnp.int32)
+    selected, nearby, candidates, wants = gather_all(keys, values, rand_blocks, glob_blocks)
     out, dq, table, own, halo = attention(
-        spots,
-        edges,
-        same,
+        rand_blocks,
+        glob_blocks,
         queries,
         d_out,
         selected.reshape(256, BLOCK, DH),
         nearby,
         candidates.reshape(24, BLOCK, DH),
     )
-
-    def owner_at(half, far, near):
-        oz = (z - jnp.where(half == 0, far, near)) % RING
-        oy = (y - jnp.where(half == 0, near, far)) % RING
-        return oz * 16 + oy * 2 + core
-
-    def lookup(ids, targets):
-        numbers = ints(32)
-        match = jnp.where(targets[None, :] == ids[:, None], numbers[:, None], NO_TERM)
-        return jnp.min(match, axis=0)
-
-    flat = ints(2 * CHUNKS * 4)
-    half, chunk = flat // (CHUNKS * 4), flat // 4 % CHUNKS
-    far = jnp.where(chunk < 24, chosen(chunk // 8, ROWS[:3]), chosen(chunk - 24, (1, -1, 2, -2)))
-    near = jnp.where(chunk < 24, chosen(chunk % 8, ORDER), 0)
-    block = owner_at(half, far, near) * 4 + flat % 4
-    theirs = partner_rand.reshape(-1)
-    index = jnp.stack([lookup(rand, block), lookup(theirs, block)])
-    flat = ints(128)
-    owner = owner_at(flat // 64, chosen(flat // 8 % 8, ROWS), chosen(flat % 8, ORDER))
-    leaf_index = jnp.stack([lookup(rand // 4, owner), lookup(theirs // 4, owner)])
-    dk, dv = scatter_all(index, leaf_index, wants, glob_blocks, table, own, halo)
+    dk, dv = scatter_all(wants, glob_blocks, table, own, halo)
+    dk, dv = pl.pallas_call(
+        copy_kernel, out_shape=[jax.ShapeDtypeStruct(dk.shape, dk.dtype)] * 2, name="write_out"
+    )(dk, dv)
     return (out, dq, dk, dv)
 
 

time: 147 us -> 127 us (0.86)
  the two profiles are of different devices: /device:TPU:24 before, /device:TPU:8 now
where the time goes in v3:
time: 127 us; the launch traced here: 126 us
  Pallas kernels  126 us (99%)
    pallas_call x1, Pallas kernels, gather_all(): pl.pallas_call(gather_kernel, out_shape=(jax.ShapeDtypeStruct((2, 2, 8, 8...  58.4 us
    pallas_call x1, Pallas kernels, scatter_all(): pl.pallas_call(scatter_kernel, out_shape=(jax.ShapeDtypeStruct((BLOCK, KV...  52.7 us
    pallas_call x1, Pallas kernels, attention(): pl.pallas_call(attention_kernel, out_shape=(jax.ShapeDtypeStruct(queries....  13.1 us

profile of v3, /device:TPU:8, one launch (start us, length us, event | category | flops | bytes accessed | tf_op | source)
XLA Modules:
  0.0 126.3 jit_solution(13156289880304503975)
XLA Ops:
  0.6 58.4 %gather_blocks.1 = (bf16[2,2,8,8,64,128]{5,4,3,2,1,0:T(8,128)(2,1)}, bf16[2,6,64,128]{3,2,1,0:T(8,128)(2,1)}, bf16[2,2,3,2,64,128]{5,4,3,2,1,0:T(8,128)(2,1)}, s32[10,1,128]{2,1,0:T(1,128)}) custom-call(bf16[64,512]{1,0:T(8,128)(2,1)} %keys.1, bf16[64,512]{1,0:T(8,128)(2,1)} %values.1, s32[4,8]{1,0:T(4,128)} %rand.3, s32[2]{0:T(128)} %glob.3), custom_call_target="tpu_custom_call" | custom-call | tf_op jit(solution)/shard_map/gather_blocks/pallas_call | solution.py:456
  59.0 13.1 %block_attention.1 = (bf16[256,1024]{1,0:T(8,128)(2,1)}, bf16[256,1024]{1,0:T(8,128)(2,1)}, bf16[2,36,64,128]{3,2,1,0:T(8,128)(2,1)}, f32[2,4,64,128]{3,2,1,0:T(8,128)}, bf16[2,2,64,128]{3,2,1,0:T(8,128)(2,1)}) custom-call(s32[4,8]{1,0:T(4,128)} %rand.3, s32[2]{0:T(128)} %glob.3, bf16[256,1024]{1,0:T(8,128)(2,1)} %queries.1, bf16[256,1024]{1,0:T(8,128)(2,1)} %d_out.1, ...), custom_call_target="tpu_custom_call" | custom-call | tf_op jit(solution)/shard_map/block_attention/pallas_call | solution.py:786
  72.1 52.7 %scatter_terms.1 = (bf16[64,512]{1,0:T(8,128)(2,1)}, bf16[64,512]{1,0:T(8,128)(2,1)}) custom-call(s32[10,1,128]{2,1,0:T(1,128)} %get-tuple-element.22.wants, s32[2]{0:T(128)} %glob.3, bf16[2,36,64,128]{3,2,1,0:T(8,128)(2,1)} %get-tuple-element.23.table, f32[2,4,64,128]{3,2,1,0:T(8,128)} %get-tuple-element.24.own, bf16[2,2,64,128]{3,2,1,0:T(8,128)(2,1)} %get-tuple-element.25.halo), custom_call_target="tpu_custom_call" | custom-call | tf_op jit(solution)/shard_map/scatter_terms/pallas_call | solution.py:654
  124.8 1.5 %write_out.1 = (bf16[64,512]{1,0:T(8,128)(2,1)}, bf16[64,512]{1,0:T(8,128)(2,1)}) custom-call(bf16[64,512]{1,0:T(8,128)(2,1)} %get-tuple-element.26.a, bf16[64,512]{1,0:T(8,128)(2,1)} %get-tuple-element.27.b), custom_call_target="tpu_custom_call" | custom-call | tf_op jit(solution)/shard_map/write_out/pallas_call | solution.py:826

commit v4 on v3

--- a/solution.py
+++ b/solution.py
@@ -36,7 +36,9 @@
 HALF_US = 0.05
 HOP_US = 2.8
 TABLE_US = 3.0
+MARGIN_US = 3.0
 KV_ROWS = 40
+PARTS = 1
 TERMS = 36
 NO_TERM = 34
 WANT = (1, 2 * RING * RING)
@@ -74,8 +76,8 @@
         name, link, time, deps = task
         free[link] = start + time
         arrival[name] = start + time + HOP_US
-        result.append(task)
-    return result, max(arrival.values())
+        result.append((start, task))
+    return result, arrival
 
 
 def far_sign(half, row):
@@ -86,7 +88,7 @@
     tasks = []
     for half in (0, 1):
         minor, major = axis_of(half, False), axis_of(half, True)
-        whole, leaf = {}, {}
+        whole = {}
         for step in range(3):
             for sign in (1, -1):
                 name = ("H", half, sign, step)
@@ -110,37 +112,34 @@
                     whole[8 * row + to] = name
         for row, sign, to, ranges in LEAVES:
             for lo, hi in ranges:
-                name = ("L", half, row, sign, to, lo, hi)
                 deps = tuple(whole[8 * row + s] for s in range(lo, hi) if row or s)
-                tasks.append((name, (major, sign), CHUNK_US * (hi - lo) / 2, deps))
-                for s in range(lo, hi):
-                    leaf[to, s] = name
+                for r in (0, 1):
+                    name = ("L", half, row, sign, to, lo, hi, r)
+                    tasks.append((name, (major, sign), CHUNK_US * (hi - lo) / 4, deps))
         copies = tuple(whole.values())
         for sign in (1, -1):
             tasks.append((("G", half, sign), (major, sign), CHUNK_US / 2, copies))
         for sign in (1, -1):
             tasks.append((("X", half, sign), "p", HALF_US, (("G", half, sign),)))
         for row in range(8):
-            groups = ((0, 5), (5, 8)) if row < 7 else ((0, 3), (3, 7), (7, 8))
+            groups = ((0, 5), (5, 8)) if row < 3 else ((0, 1),) if row < 7 else ()
             for lo, hi in groups:
-                deps = []
-                for s in range(lo, hi):
-                    if row < 3:
-                        deps.append(whole.get(8 * row + s))
-                    elif row < 7 and s == 0:
-                        deps.append(whole[PATH[ROWS[row]]])
-                    else:
-                        deps.append(leaf[row, s])
-                deps = tuple(dict.fromkeys(d for d in deps if d))
+                if row < 3:
+                    deps = tuple(whole[8 * row + s] for s in range(lo, hi) if row or s)
+                else:
+                    deps = (whole[PATH[ROWS[row]]],)
                 tasks.append((("P", half, row, lo, hi), "p", HALF_US * (hi - lo), deps))
-    late = [task for task in ordered(tasks)[0] if task[0][0] in "PX"]
+    late = [task for _, task in ordered(tasks)[0] if task[0][0] in "PX"]
+    main, arrival = ordered([task for task in tasks if task[0][0] not in "PX"])
     result, seen = [], set()
-    for task in ordered([task for task in tasks if task[0][0] not in "PX"])[0]:
+    for start, task in main:
+        for other in [t for t in late if t[0][0] == "P"]:
+            if set(other[3]) <= seen or max(arrival[d] for d in other[3]) + MARGIN_US < start:
+                late.remove(other)
+                result.append(other)
+                seen.update(other[3])
         result.append(task)
         seen.update(task[3])
-        for other in [t for t in late if set(t[3]) <= seen]:
-            late.remove(other)
-            result.append(other)
     return result + late
 
 
@@ -170,8 +169,7 @@
                 major = axis_of(half, True)
                 for r in (0, 1):
                     name = ("L", half, to, sign, lo, hi, r)
-                    deps = (("T", 0),) if r else ()
-                    tasks.append((name, (major, -sign), CHUNK_US * (hi - lo) / 4, deps))
+                    tasks.append((name, (major, -sign), CHUNK_US * (hi - lo) / 4, ()))
                     for s in range(lo, hi):
                         leaf[half, to, s, r] = name
     for half in (0, 1):
@@ -200,7 +198,7 @@
         deps = tuple((k, half, s, 1) for k in "H" for s in (1, -1))
         deps += (("m", half, 0, 1, 1), ("m", half, 0, -1, 1))
         tasks.append((("F", half), ("f", half), 0.0, deps))
-    return ordered(tasks)[0]
+    return [task for _, task in ordered(tasks)[0]]
 
 
 GATHER = gather_tasks()
@@ -272,6 +270,8 @@
 
 SLOTS_MOD = [SLOT[d] if d <= 4 else SLOT[d - RING] for d in range(RING)]
 ROWS_MOD = [ROWS.index(d) if d <= 4 else ROWS.index(d - RING) for d in range(RING)]
+SLOTS_PACKED = sum(v << (3 * d) for d, v in enumerate(SLOTS_MOD))
+ROWS_PACKED = sum(v << (3 * d) for d, v in enumerate(ROWS_MOD))
 PARENT = [0, 0, 0, 2, 1, 1, 2, 2]
 
 
@@ -392,13 +392,13 @@
             src = full[half].at[8 * row + SLOT[sign * step]]
             dst = full[half].at[8 * row + (7 if step == 3 else SLOT[sign * (step + 1)])]
         elif kind == "L":
-            _, _, row, sign, to, lo, hi = name
+            _, _, row, sign, to, lo, hi, r = name
             side = SIDES[major, sign] * 2
             for s in range(lo, hi):
-                for r in (0, 1):
-                    staged[half, r, to, s] = pick(half, 8 * row + s, side + r)
-            src = staged.at[half, :, to, pl.ds(lo, hi - lo)]
-            dst = picked.at[half, :, to, pl.ds(lo, hi - lo)]
+                staged[half, r, to, s] = pick(half, 8 * row + s, side + r)
+            src = staged.at[half, r, to, pl.ds(lo, hi - lo)]
+            dst = sel_out.at[r, half, to, pl.ds(lo, hi - lo)]
+            peer = peers[major, sign, r]
         elif kind == "P":
             _, _, row, lo, hi = name
             for s in range(lo, hi):
@@ -565,8 +565,8 @@
         elif kind == "L":
             _, _, to, sign, lo, hi, r = name
             for s in range(lo, hi):
-                owner = owner_of(half, z, y, core, ROWS[to], ORDER[s])
-                staged[half, r, to, s] = (table, mirror)[r][half, wants[8 + r, 0, owner] // 4]
+                owner = owner_of(half, z, y, 1 - core if r else core, ROWS[to], ORDER[s])
+                staged[half, r, to, s] = table[half, wants[8, 0, owner] // 4]
             span = pl.ds(lo, hi - lo)
             src, dst = staged.at[half, r, to, span], landed.at[half, r, to, span]
         elif kind == "m":
@@ -614,7 +614,7 @@
             else:
                 dst = stem.at[half, 0 if sign > 0 else 1]
         i = SCATTER_SENDS[name]
-        peer = peers["p"] if link == "p" else peers[link[0], link[1], 0]
+        peer = peers["p"] if link == "p" else peers[link[0], link[1], name[6] if kind == "L" else 0]
         copy = remote(src, dst, send.at[i], recv.at[i], peer)
         copy.start()
         started[name] = copy
@@ -687,13 +687,12 @@
 ):
     seq, _, z, y, core = place()
     copies = [pltpu.make_async_copy(nearby.at[n], kv.at[n, pl.ds(0, 6)], gsems.at[n]) for n in (0, 1)]
-    for e in range(4 * RAND):
-        owner = rand[e // RAND, e % RAND] // 4
-        away = (owner + core) % 2
-        for n in (0, 1):
-            row, slot = relation(z, y, owner, n)
-            spot = ((away * 2 + n) * 8 + row) * 8 + slot
-            copies.append(pltpu.make_async_copy(selected.at[spot], kv.at[n, 8 + e], sems.at[n, e]))
+    for copy in copies:
+        copy.start()
+
+    def fetch(n, e, spot):
+        return pltpu.make_async_copy(selected.at[spot], kv.at[n, 8 + e], sems.at[n, e])
+
     for k in (0, 1):
         owner = ids[k] // 4
         away = (owner + core) % 2
@@ -707,8 +706,18 @@
             copies.append(
                 pltpu.make_async_copy(candidates.at[spot], kv.at[n, 6 + k], gsems.at[2 + 2 * n + k])
             )
-    for copy in copies:
-        copy.start()
+            copies[-1].start()
+    def start_fetches(i, e):
+        owner = rand[i, e] // 4
+        away = (owner + core) % 2
+        dz = 3 * ((z + RING - owner // 16) % RING)
+        dy = 3 * ((y + RING - (owner // 2) % RING) % RING)
+        for n, far, near_by in ((0, dz, dy), (1, dy, dz)):
+            at = ((ROWS_PACKED >> far) & 7) * 8 + ((SLOTS_PACKED >> near_by) & 7)
+            fetch(n, i * RAND + e, (away * 2 + n) * 64 + at).start()
+
+    for e in range(RAND):
+        start_fetches(0, e)
     near[...] = jnp.zeros_like(near)
     glob[...] = jnp.zeros_like(glob)
     for n in (0, 1):
@@ -721,14 +730,13 @@
     def dot(a, b, at, bt):
         return lax.dot_general(a, b, dims(at, bt), preferred_element_type=F32)
 
-    @pl.loop(0, 4)
-    def _(i):
-        rows = pl.ds(pl.multiple_of(i * BLOCK, BLOCK), BLOCK)
-        stack = lambda ref: jnp.concatenate(
-            [ref[rows, h * DH : (h + 1) * DH] for h in range(HEADS)], axis=0
-        )
-        q, g = stack(queries), stack(d_out)
-
+    for i in range(4):
+        for e in range(RAND):
+            for n in (0, 1):
+                fetch(n, i * RAND + e, 0).wait()
+            if i < 3:
+                start_fetches(i + 1, e)
+        rows = pl.ds(i * BLOCK, BLOCK)
         def listed(n):
             return jnp.concatenate(
                 [
@@ -740,32 +748,39 @@
             )
 
         k, v = listed(0), listed(1)
-        scores = dot(k, q, 1, 1) * factor
         cut_first = jnp.logical_and(i == 0, seq == 0)
         cut_last = jnp.logical_and(i == 3, seq == lax.axis_size("seq") - 1)
-        scores = jnp.concatenate(
-            [
-                jnp.where(cut_first, NEG_FILL, scores[:BLOCK]),
-                scores[BLOCK : 2 * BLOCK],
-                jnp.where(cut_last, NEG_FILL, scores[2 * BLOCK : 3 * BLOCK]),
-                scores[3 * BLOCK :],
-            ],
-            axis=0,
-        )
-        peak = jnp.max(scores, axis=0, keepdims=True)
-        weights = jnp.exp(scores - peak)
-        probs = weights * (1.0 / jnp.sum(weights, axis=0, keepdims=True))
-        probs16 = probs.astype(BF16)
-        result = dot(v, probs16, 0, 0).astype(BF16)
-        delta = jnp.sum(g.T.astype(F32) * result.astype(F32), axis=0, keepdims=True)
-        dprobs = dot(v, g, 1, 1)
-        dscores = (probs * (dprobs - delta)).astype(BF16)
-        dquery = (dot(k, dscores, 0, 0) * factor).astype(BF16).T
-        result = result.T
-        for h in range(HEADS):
-            out[rows, h * DH : (h + 1) * DH] = result[h * BLOCK : (h + 1) * BLOCK]
-            dq[rows, h * DH : (h + 1) * DH] = dquery[h * BLOCK : (h + 1) * BLOCK]
-        for n, terms in ((0, dot(dscores, q, 1, 0) * factor), (1, dot(probs16, g, 1, 0))):
+        sums = [None, None]
+        for part in range(PARTS):
+            heads = range(part * HEADS // PARTS, (part + 1) * HEADS // PARTS)
+            stack = lambda ref: jnp.concatenate([ref[rows, h * DH : (h + 1) * DH] for h in heads], axis=0)
+            q, g = stack(queries), stack(d_out)
+            scores = dot(k, q, 1, 1) * factor
+            scores = jnp.concatenate(
+                [
+                    jnp.where(cut_first, NEG_FILL, scores[:BLOCK]),
+                    scores[BLOCK : 2 * BLOCK],
+                    jnp.where(cut_last, NEG_FILL, scores[2 * BLOCK : 3 * BLOCK]),
+                    scores[3 * BLOCK :],
+                ],
+                axis=0,
+            )
+            peak = jnp.max(scores, axis=0, keepdims=True)
+            weights = jnp.exp(scores - peak)
+            probs = weights * (1.0 / jnp.sum(weights, axis=0, keepdims=True))
+            probs16 = probs.astype(BF16)
+            result = dot(v, probs16, 0, 0).astype(BF16)
+            delta = jnp.sum(g.T.astype(F32) * result.astype(F32), axis=0, keepdims=True)
+            dprobs = dot(v, g, 1, 1)
+            dscores = (probs * (dprobs - delta)).astype(BF16)
+            dquery = (dot(k, dscores, 0, 0) * factor).astype(BF16).T
+            result = result.T
+            for n, h in enumerate(heads):
+                out[rows, h * DH : (h + 1) * DH] = result[n * BLOCK : (n + 1) * BLOCK]
+                dq[rows, h * DH : (h + 1) * DH] = dquery[n * BLOCK : (n + 1) * BLOCK]
+            for n, terms in ((0, dot(dscores, q, 1, 0)), (1, dot(probs16, g, 1, 0))):
+                sums[n] = terms if sums[n] is None else sums[n] + terms
+        for n, terms in ((0, sums[0] * factor), (1, sums[1])):
             near[n, pl.ds(i, 3)] += terms[: 3 * BLOCK].reshape(3, BLOCK, DH)
             glob[n] += terms[3 * BLOCK : 5 * BLOCK].reshape(2, BLOCK, DH)
             table[n, pl.ds(i * RAND, RAND)] = terms[5 * BLOCK :].astype(BF16).reshape(RAND, BLOCK, DH)

time: 127 us -> 126 us (level)
  the two profiles are of different devices: /device:TPU:8 before, /device:TPU:1 now
where the time goes in v4:
time: 126 us
  Pallas kernels  125 us (99%)
    pallas_call x1, Pallas kernels, gather_all(): pl.pallas_call(gather_kernel, out_shape=(jax.ShapeDtypeStruct((2, 2, 8, 8...  61.1 us
    pallas_call x1, Pallas kernels, scatter_all(): pl.pallas_call(scatter_kernel, out_shape=(jax.ShapeDtypeStruct((BLOCK, KV...  50.1 us
    pallas_call x1, Pallas kernels, attention(): pl.pallas_call(attention_kernel, out_shape=(jax.ShapeDtypeStruct(queries....  12.7 us

profile of v4, /device:TPU:1, one launch (start us, length us, event | category | flops | bytes accessed | tf_op | source)
XLA Modules:
  0.0 126.1 jit_solution(13879279993421879349)
XLA Ops:
  0.6 61.1 %gather_blocks.1 = (bf16[2,2,8,8,64,128]{5,4,3,2,1,0:T(8,128)(2,1)}, bf16[2,6,64,128]{3,2,1,0:T(8,128)(2,1)}, bf16[2,2,3,2,64,128]{5,4,3,2,1,0:T(8,128)(2,1)}, s32[10,1,128]{2,1,0:T(1,128)}) custom-call(bf16[64,512]{1,0:T(8,128)(2,1)} %keys.1, bf16[64,512]{1,0:T(8,128)(2,1)} %values.1, s32[4,8]{1,0:T(4,128)} %rand.3, s32[2]{0:T(128)} %glob.3), custom_call_target="tpu_custom_call" | custom-call | tf_op jit(solution)/shard_map/gather_blocks/pallas_call | solution.py:456
  61.7 12.7 %block_attention.1 = (bf16[256,1024]{1,0:T(8,128)(2,1)}, bf16[256,1024]{1,0:T(8,128)(2,1)}, bf16[2,36,64,128]{3,2,1,0:T(8,128)(2,1)}, f32[2,4,64,128]{3,2,1,0:T(8,128)}, bf16[2,2,64,128]{3,2,1,0:T(8,128)(2,1)}) custom-call(s32[4,8]{1,0:T(4,128)} %rand.3, s32[2]{0:T(128)} %glob.3, bf16[256,1024]{1,0:T(8,128)(2,1)} %queries.1, bf16[256,1024]{1,0:T(8,128)(2,1)} %d_out.1, ...), custom_call_target="tpu_custom_call" | custom-call | tf_op jit(solution)/shard_map/block_attention/pallas_call | solution.py:801
  74.5 50.1 %scatter_terms.1 = (bf16[64,512]{1,0:T(8,128)(2,1)}, bf16[64,512]{1,0:T(8,128)(2,1)}) custom-call(s32[10,1,128]{2,1,0:T(1,128)} %get-tuple-element.22.wants, s32[2]{0:T(128)} %glob.3, bf16[2,36,64,128]{3,2,1,0:T(8,128)(2,1)} %get-tuple-element.23.table, f32[2,4,64,128]{3,2,1,0:T(8,128)} %get-tuple-element.24.own, bf16[2,2,64,128]{3,2,1,0:T(8,128)(2,1)} %get-tuple-element.25.halo), custom_call_target="tpu_custom_call" | custom-call | tf_op jit(solution)/shard_map/scatter_terms/pallas_call | solution.py:654
  124.6 1.5 %write_out.1 = (bf16[64,512]{1,0:T(8,128)(2,1)}, bf16[64,512]{1,0:T(8,128)(2,1)}) custom-call(bf16[64,512]{1,0:T(8,128)(2,1)} %get-tuple-element.26.a, bf16[64,512]{1,0:T(8,128)(2,1)} %get-tuple-element.27.b), custom_call_target="tpu_custom_call" | custom-call | tf_op jit(solution)/shard_map/write_out/pallas_call | solution.py:841

commit v5 on v4

--- a/solution.py
+++ b/solution.py
@@ -169,7 +169,8 @@
                 major = axis_of(half, True)
                 for r in (0, 1):
                     name = ("L", half, to, sign, lo, hi, r)
-                    tasks.append((name, (major, -sign), CHUNK_US * (hi - lo) / 4, ()))
+                    deps = (("T", 0),) if r else ()
+                    tasks.append((name, (major, -sign), CHUNK_US * (hi - lo) / 4, deps))
                     for s in range(lo, hi):
                         leaf[half, to, s, r] = name
     for half in (0, 1):
@@ -565,8 +566,8 @@
         elif kind == "L":
             _, _, to, sign, lo, hi, r = name
             for s in range(lo, hi):
-                owner = owner_of(half, z, y, 1 - core if r else core, ROWS[to], ORDER[s])
-                staged[half, r, to, s] = table[half, wants[8, 0, owner] // 4]
+                owner = owner_of(half, z, y, core, ROWS[to], ORDER[s])
+                staged[half, r, to, s] = (table, mirror)[r][half, wants[8 + r, 0, owner] // 4]
             span = pl.ds(lo, hi - lo)
             src, dst = staged.at[half, r, to, span], landed.at[half, r, to, span]
         elif kind == "m":
@@ -614,7 +615,7 @@
             else:
                 dst = stem.at[half, 0 if sign > 0 else 1]
         i = SCATTER_SENDS[name]
-        peer = peers["p"] if link == "p" else peers[link[0], link[1], name[6] if kind == "L" else 0]
+        peer = peers["p"] if link == "p" else peers[link[0], link[1], 0]
         copy = remote(src, dst, send.at[i], recv.at[i], peer)
         copy.start()
         started[name] = copy

time: 126 us -> 126 us (level)
  the two profiles are of different devices: /device:TPU:1 before, /device:TPU:24 now
where the time goes in v5:
time: 126 us
  Pallas kernels  125 us (99%)
    pallas_call x1, Pallas kernels, gather_all(): pl.pallas_call(gather_kernel, out_shape=(jax.ShapeDtypeStruct((2, 2, 8, 8...  57.9 us
    pallas_call x1, Pallas kernels, scatter_all(): pl.pallas_call(scatter_kernel, out_shape=(jax.ShapeDtypeStruct((BLOCK, KV...  53.3 us
    pallas_call x1, Pallas kernels, attention(): pl.pallas_call(attention_kernel, out_shape=(jax.ShapeDtypeStruct(queries....  12.7 us

profile of v5, /device:TPU:24, one launch (start us, length us, event | category | flops | bytes accessed | tf_op | source)
XLA Modules:
  0.0 126.1 jit_solution(16575836295535749711)
XLA Ops:
  0.6 57.9 %gather_blocks.1 = (bf16[2,2,8,8,64,128]{5,4,3,2,1,0:T(8,128)(2,1)}, bf16[2,6,64,128]{3,2,1,0:T(8,128)(2,1)}, bf16[2,2,3,2,64,128]{5,4,3,2,1,0:T(8,128)(2,1)}, s32[10,1,128]{2,1,0:T(1,128)}) custom-call(bf16[64,512]{1,0:T(8,128)(2,1)} %keys.1, bf16[64,512]{1,0:T(8,128)(2,1)} %values.1, s32[4,8]{1,0:T(4,128)} %rand.3, s32[2]{0:T(128)} %glob.3), custom_call_target="tpu_custom_call" | custom-call | tf_op jit(solution)/shard_map/gather_blocks/pallas_call | solution.py:457
  58.6 12.7 %block_attention.1 = (bf16[256,1024]{1,0:T(8,128)(2,1)}, bf16[256,1024]{1,0:T(8,128)(2,1)}, bf16[2,36,64,128]{3,2,1,0:T(8,128)(2,1)}, f32[2,4,64,128]{3,2,1,0:T(8,128)}, bf16[2,2,64,128]{3,2,1,0:T(8,128)(2,1)}) custom-call(s32[4,8]{1,0:T(4,128)} %rand.3, s32[2]{0:T(128)} %glob.3, bf16[256,1024]{1,0:T(8,128)(2,1)} %queries.1, bf16[256,1024]{1,0:T(8,128)(2,1)} %d_out.1, ...), custom_call_target="tpu_custom_call" | custom-call | tf_op jit(solution)/shard_map/block_attention/pallas_call | solution.py:802
  71.3 53.3 %scatter_terms.1 = (bf16[64,512]{1,0:T(8,128)(2,1)}, bf16[64,512]{1,0:T(8,128)(2,1)}) custom-call(s32[10,1,128]{2,1,0:T(1,128)} %get-tuple-element.22.wants, s32[2]{0:T(128)} %glob.3, bf16[2,36,64,128]{3,2,1,0:T(8,128)(2,1)} %get-tuple-element.23.table, f32[2,4,64,128]{3,2,1,0:T(8,128)} %get-tuple-element.24.own, bf16[2,2,64,128]{3,2,1,0:T(8,128)(2,1)} %get-tuple-element.25.halo), custom_call_target="tpu_custom_call" | custom-call | tf_op jit(solution)/shard_map/scatter_terms/pallas_call | solution.py:655
  124.6 1.5 %write_out.1 = (bf16[64,512]{1,0:T(8,128)(2,1)}, bf16[64,512]{1,0:T(8,128)(2,1)}) custom-call(bf16[64,512]{1,0:T(8,128)(2,1)} %get-tuple-element.26.a, bf16[64,512]{1,0:T(8,128)(2,1)} %get-tuple-element.27.b), custom_call_target="tpu_custom_call" | custom-call | tf_op jit(solution)/shard_map/write_out/pallas_call | solution.py:842
